TPU v7x, 256 devices: a whole 4x4x8 slice. The times are simulated.
256 devices in a mesh: rows: 64 (over z, x, core), cols: 4 (over y).
Axes of the slice: x: 4, y: 4, z: 8, core: 2. Of those that a mesh axis runs over, the one named last changes fastest.
Arguments:
- h_blocks: float32 [512, 48, 64, 64], P('rows', 'cols'), may hold values from -0.109375 to 0.109375
- p_blocks: float32 [512, 48, 64, 64], P('rows', 'cols'), may hold values from -0.109375 to 0.109375
- h_fetch: int32 [64, 64, 2], P('rows'), may hold values from 0 to 7
- p_fetch: int32 [64, 64, 2], P('rows'), may hold values from 0 to 7
- h_slot: int32 [512, 48], P('rows'), may hold values from 0 to 127
- p_slot: int32 [512, 48], P('rows'), may hold values from 0 to 127
- p_panel: float32 [32768, 1024], P('rows', 'cols'), may hold values from -6 to 6
Outputs:
- w_panel: float32 [32768, 1024], P('rows', 'cols')
Inputs may be any that keep to these rules, and one draw needn't show every extreme that they name: `p_fetch`: local block rows of the owner. `h_slot`: slot 2 * o + c names entry c of the owner o's fetch list. `p_slot`: slot 2 * o + c names entry c of the owner o's fetch list.
All inputs are finite; a program needn't handle non-finite values.
Results may differ from a plain program's by a relative error of at most 0.000098.
Values sent between devices are 32-bit elements; how exact they have to be, the bound alone decides.
No kernel may reach another device: no remote copies, remote signals or barrier semaphores. Data moves between devices by JAX's collectives and lax.ppermute only.
A program may use at most 128 MiB of HBM per device.

v0:
```python
import functools

import jax
import jax.numpy as jnp
from jax import lax
from jax.experimental import pallas as pl
from jax.experimental.pallas import tpu as pltpu
from jax.sharding import PartitionSpec as P

NZ, NX, NC, NY = 8, 4, 2, 4
B, HALF = 64, 128
GROUPS = ((0,), (7, 1), (6, 2), (5, 3, 4))

WHOLE = (False, True, False, True)


def rows_shift(array, dz=0, dx=0, dc=0):
    pairs = []
    for z in range(NZ):
        for x in range(NX):
            for c in range(NC):
                target = (((z + dz) % NZ) * NX + (x + dx) % NX) * NC + (c ^ dc)
                pairs.append(((z * NX + x) * NC + c, target))
    return lax.ppermute(array, "rows", pairs)


def cols_shift(array, dy):
    return lax.ppermute(array, "cols", [(y, (y + dy) % NY) for y in range(NY)])


def x_exchange(array):
    groups = [[(z * NX + x) * NC + c for x in range(NX)] for z in range(NZ) for c in range(NC)]
    return lax.all_to_all(array, "rows", 0, 0, axis_index_groups=groups, tiled=True)


def pack_kernel(offsets, whole, meta, fetch, *refs):
    pieces, outs = refs[: len(offsets)], refs[len(offsets) :]
    z, x, c = meta[0], meta[1], meta[2]
    for n, off in enumerate(offsets):
        base = (((z + off) & 7) * NX + x) * 4
        for s in range(NX):
            for j in range(8):
                cc, l, f = j >> 2, (j >> 1) & 1, j & 1
                row = cc * 8 + fetch[s * 2 + l, base + (c ^ cc) * 2 + f]
                if whole:
                    outs[0][(x + s) & 3, n * 8 + j] = pieces[n][row]
                else:
                    outs[s][n * 8 + j] = pieces[n][row]


def pack(offsets, whole, meta, fetch, pieces):
    part = (len(offsets) * 8,) + pieces[0].shape[1:]
    shapes = [(NX,) + part] if whole else [part] * NX
    return pl.pallas_call(
        functools.partial(pack_kernel, offsets, whole),
        out_shape=[jax.ShapeDtypeStruct(shape, jnp.float32) for shape in shapes],
        grid_spec=pltpu.PrefetchScalarGridSpec(
            num_scalar_prefetch=2,
            grid=(1,),
            in_specs=[pl.BlockSpec(pieces[0].shape, lambda *_: (0, 0, 0))] * len(pieces),
            out_specs=[pl.BlockSpec(shape, lambda *_, k=len(shape): (0,) * k) for shape in shapes],
        ),
        name="pack",
    )(meta, fetch, *pieces)


def product_kernel(meta, pos, *refs):
    arrived = iter(refs[2:-4])
    out, slabs, split, sems = refs[-4:]
    x, y = meta[1], meta[3]
    step = pl.program_id(0)

    @pl.when(step == 0)
    def _():
        for g, offsets in enumerate(GROUPS):
            block = next(arrived) if WHOLE[g] else None
            for s in range(NX):
                xp = (x - s) & 3
                part = block.at[xp] if WHOLE[g] else next(arrived)
                for n, off in enumerate(offsets):
                    pltpu.make_async_copy(
                        part.at[pl.ds(n * 8, 8)], slabs.at[pl.ds((xp * NZ + off) * 8, 8)], sems.at[xp]
                    ).start()
        for xp in range(NX):
            part = slabs.at[pl.ds(xp * 64, 64)]
            pltpu.make_async_copy(part, part, sems.at[xp]).wait()

            def convert(i, carry):
                value = slabs[i]
                high = value.astype(jnp.bfloat16)
                split[i, :, :HALF] = high
                split[i, :, HALF:] = (value - high.astype(jnp.float32)).astype(jnp.bfloat16)
                return carry

            lax.fori_loop(xp * 64, xp * 64 + 64, convert, 0, unroll=4)

    for l, blocks in enumerate(refs[:2]):
        total = jnp.zeros((2 * B, 2 * HALF), jnp.float32)
        for q, off in enumerate((0, 3, 1, 2)):
            base = (l * 8 + step) * 48 + ((y + off) % NY) * 12
            left = blocks[q, 0]
            high = left.astype(jnp.bfloat16)
            low = (left - high.astype(jnp.float32)).astype(jnp.bfloat16)
            right = jnp.concatenate([split[pos[base + j]] for j in range(12)], axis=0)
            total = total + jnp.dot(
                jnp.concatenate([high, low], axis=0), right, preferred_element_type=jnp.float32
            )
        upper, lower = total[:B], total[B:]
        out[l, 0] = upper[:, :HALF] + (upper[:, HALF:] + (lower[:, :HALF] + lower[:, HALF:]))


def product(meta, pos, own_blocks, partner_blocks, arrived):
    block = pl.BlockSpec((4, 1, B, 768), lambda i, *_: (0, i, 0, 0))
    anywhere = pl.BlockSpec(memory_space=pl.ANY)
    return pl.pallas_call(
        product_kernel,
        out_shape=jax.ShapeDtypeStruct((2, 8, B, HALF), jnp.float32),
        grid_spec=pltpu.PrefetchScalarGridSpec(
            num_scalar_prefetch=2,
            grid=(8,),
            in_specs=[block] * 2 + [anywhere] * len(arrived),
            out_specs=pl.BlockSpec((2, 1, B, HALF), lambda i, *_: (0, i, 0, 0)),
            scratch_shapes=[
                pltpu.VMEM((256, B, HALF), jnp.float32),
                pltpu.VMEM((256, B, 2 * HALF), jnp.bfloat16),
                pltpu.SemaphoreType.DMA((NX,)),
            ],
        ),
        name="product",
    )(meta, pos, own_blocks, partner_blocks, *arrived)


def fetch_rows(own, meta, fetch_x):
    line = {0: own}
    up = down = own
    for n in range(1, 4):
        up = rows_shift(up, dz=1)
        down = rows_shift(down, dz=-1)
        line[NZ - n], line[n] = up, down
    line[4] = rows_shift(up, dz=1)
    arrived = []
    for g, offsets in enumerate(GROUPS):
        packed = pack(offsets, WHOLE[g], meta, fetch_x, [line[off] for off in offsets])
        if WHOLE[g]:
            arrived.append(x_exchange(packed[0]))
            continue
        arrived.append(packed[0])
        for s in range(1, NX):
            arrived.append(rows_shift(packed[s], dx=s))
    return arrived


def turn_kernel(blocks, out):
    for t in range(6):
        out[0, :, t * 128 : (t + 1) * 128] = jnp.concatenate([blocks[0, 2 * t], blocks[0, 2 * t + 1]], axis=1)


def gather_blocks(blocks, halves):
    mine = pl.pallas_call(
        turn_kernel,
        out_shape=jax.ShapeDtypeStruct((8, B, 768), jnp.float32),
        grid=(8,),
        in_specs=[pl.BlockSpec((1, 12, B, B), lambda i: (i, 0, 0, 0))],
        out_specs=pl.BlockSpec((1, B, 768), lambda i: (i, 0, 0)),
        name="turn",
    )(blocks)
    own = [mine]
    for dy in (1, -1, 2)[: 2 if halves else 3]:
        own.append(cols_shift(mine, dy))
    if halves:
        far = []
        for n, dy in enumerate((1, -1)):
            far.append(cols_shift(own[n + 1][n * 4 : n * 4 + 4], dy))
        own.append(jnp.concatenate(far, axis=0))
    return own


def with_partner(own):
    own = jnp.stack(own)
    return own, rows_shift(own, dc=1)


def positions(slots, z, c):
    owner, f = slots // 2, slots % 2
    zp, xp, cp = owner // 8, (owner // 2) % 4, owner % 2
    l = lax.broadcasted_iota(jnp.int32, slots.shape, 0) // 8
    return ((xp * NZ + (zp - z) % NZ) * 8 + (cp ^ c) * 4 + l * 2 + f).reshape(-1)


def body(h_blocks, p_blocks, h_fetch, p_fetch, h_slot, p_slot, p_panel):
    r = lax.axis_index("rows").astype(jnp.int32)
    z, x, c = r // 8, (r // 2) % 4, r % 2
    meta = jnp.stack([z, x, c, lax.axis_index("cols").astype(jnp.int32)])

    pad = ((0, 0), (0, 80))
    numbers = jnp.concatenate(
        [h_fetch.reshape(1, 128), p_fetch.reshape(1, 128), jnp.pad(h_slot, pad), jnp.pad(p_slot, pad)], axis=0
    )
    other = rows_shift(numbers, dc=1)
    lists = jnp.concatenate([numbers[:2], other[:2]], axis=0)
    along = [lists] + [rows_shift(lists, dx=-s) for s in range(1, 4)]

    left, right = p_panel[:, :HALF], p_panel[:, HALF:]
    keep, give = jnp.where(c == 0, left, right), jnp.where(c == 0, right, left)
    given = rows_shift(give, dc=1)
    own = jnp.concatenate([keep, given], axis=0).reshape(16, B, HALF)

    blocks = [gather_blocks(h_blocks, True), gather_blocks(p_blocks, False)]

    for n in range(2):
        fetch_x = jnp.concatenate([a[n::2] for a in along], axis=0)
        low = 2 + 8 * n
        pos = positions(jnp.concatenate([numbers[low : low + 8, :48], other[low : low + 8, :48]], axis=0), z, c)
        arrived = fetch_rows(own, meta, fetch_x)
        own = product(meta, pos, *with_partner(blocks[n]), arrived).reshape(16, B, HALF)

    result = own.reshape(2, 512, HALF)
    back = rows_shift(result[1], dc=1)
    return jnp.where(
        c == 0,
        jnp.concatenate([result[0], back], axis=1),
        jnp.concatenate([back, result[0]], axis=1),
    )


def solution(mesh):
    in_specs = (
        P("rows", "cols", None, None),
        P("rows", "cols", None, None),
        P("rows", None, None),
        P("rows", None, None),
        P("rows", None),
        P("rows", None),
        P("rows", "cols"),
    )
    return jax.shard_map(body, mesh=mesh, in_specs=in_specs, out_specs=P("rows", "cols"), check_vma=False)
```

profile of v0, /device:TPU:16, one launch (start us, length us, event | category | flops | bytes accessed | tf_op | source)
XLA Modules:
  0.0 411.0 jit_solution(17380089460396483795)
XLA Ops:
  0.0 6.1 %turn.3 = f32[8,64,768]{2,1,0:T(8,128)} custom-call(f32[8,12,64,64]{3,2,1,0:T(8,128)} %blocks.3), custom_call_target="tpu_custom_call" | custom-call | tf_op jit(solution)/shard_map/turn/pallas_call | solution.py:159
  8.1 34.3 %collective-permute-done.8 = f32[8,64,768]{2,1,0:T(8,128)S(1)} collective-permute-done((f32[8,64,768]{2,1,0:T(8,128)}, f32[8,64,768]{2,1,0:T(8,128)S(1)}, u32[]{:S(2)}, u32[]{:S(2)}) %collective-permute-start.8) | collective-permute-done | bytes 1572896 | tf_op jit(solution)/shard_map/ppermute | solution.py:28
  44.8 16.3 %collective-permute-done.10 = f32[4,64,768]{2,1,0:T(8,128)S(1)} collective-permute-done((f32[4,64,768]{2,1,0:T(8,128)S(1)}, f32[4,64,768]{2,1,0:T(8,128)S(1)}, u32[]{:S(2)}, u32[]{:S(2)}) %collective-permute-start.10) | collective-permute-done | bytes 786464 | tf_op jit(solution)/shard_map/ppermute | solution.py:28
  62.4 3.0 pad_maximum_fusion.1.refs_0_
  66.0 10.1 %collective-permute-done.13 = f32[512,128]{1,0:T(8,128)S(1)} collective-permute-done((f32[512,128]{1,0:T(8,128)S(1)}, f32[512,128]{1,0:T(8,128)S(1)}, u32[]{:S(2)}, u32[]{:S(2)}) %collective-permute-start.13) | collective-permute-done | bytes 262176 | tf_op jit(solution)/shard_map/ppermute | solution.py:24
  76.1 2.0 collective-permute-start.17
  78.1 4.0 collective-permute-start.18
  82.1 12.1 %collective-permute-done.17.refs_0_ = f32[16,64,128]{2,1,0:T(8,128)S(1)} collective-permute-done((f32[16,64,128]{2,1,0:T(8,128)S(1)}, f32[16,64,128]{2,1,0:T(8,128)S(1)}, u32[]{:S(2)}, u32[]{:S(2)}) %collective-permute-start.17) | collective-permute-done | bytes 524320 | tf_op jit(solution)/shard_map/ppermute | solution.py:24
  94.8 3.3 collective-permute-start.20
  99.4 2.8 collective-permute-start.5
  105.2 2.2 collective-permute-done.6
  109.5 3.4 pack.9
  112.9 4.3 %all-to-all-start = ((f32[4,16,64,128]{3,2,1,0:T(8,128)}), f32[4,16,64,128]{3,2,1,0:T(8,128)S(1)}, u32[]{:S(2)}, u32[]{:S(2)}) async-start(f32[4,16,64,128]{3,2,1,0:T(8,128)} %pack.9), calls=%async_computation | async-start | bytes 4194304 | tf_op jit(solution)/shard_map/all_to_all | solution.py:33
  117.2 6.1 %turn.2 = f32[8,64,768]{2,1,0:T(8,128)} custom-call(f32[8,12,64,64]{3,2,1,0:T(8,128)} %blocks.2), custom_call_target="tpu_custom_call" | custom-call | tf_op jit(solution)/shard_map/turn/pallas_call | solution.py:159
  123.3 2.9 collective-permute-start.1
  126.2 2.2 collective-permute-start.3
  128.4 3.2 collective-permute-start.25
  131.6 8.8 %collective-permute-done.25.refs_1_ = f32[16,64,128]{2,1,0:T(8,128)S(1)} collective-permute-done((f32[16,64,128]{2,1,0:T(8,128)S(1)}, f32[16,64,128]{2,1,0:T(8,128)S(1)}, u32[]{:S(2)}, u32[]{:S(2)}) %collective-permute-start.25) | collective-permute-done | bytes 524320 | tf_op jit(solution)/shard_map/ppermute | solution.py:24
  140.4 12.7 %collective-permute-done.26.refs_2_ = f32[16,64,128]{2,1,0:T(8,128)} collective-permute-done((f32[16,64,128]{2,1,0:T(8,128)}, f32[16,64,128]{2,1,0:T(8,128)}, u32[]{:S(2)}, u32[]{:S(2)}) %collective-permute-start.26) | collective-permute-done | bytes 524320 | tf_op jit(solution)/shard_map/ppermute | solution.py:24
  153.1 3.9 pack.11
  158.4 4.2 %all-to-all-start.1 = ((f32[4,24,64,128]{3,2,1,0:T(8,128)}), f32[4,24,64,128]{3,2,1,0:T(8,128)S(1)}, u32[]{:S(2)}, u32[]{:S(2)}) async-start(f32[4,24,64,128]{3,2,1,0:T(8,128)} %pack.11), calls=%async_computation.1 | async-start | bytes 6291456 | tf_op jit(solution)/shard_map/all_to_all | solution.py:33
  163.8 28.7 %collective-permute-done.3 = f32[8,64,768]{2,1,0:T(8,128)} collective-permute-done((f32[8,64,768]{2,1,0:T(8,128)}, f32[8,64,768]{2,1,0:T(8,128)}, u32[]{:S(2)}, u32[]{:S(2)}) %collective-permute-start.3) | collective-permute-done | bytes 1572896 | tf_op jit(solution)/shard_map/ppermute | solution.py:28
  192.5 4.7 %pad_maximum_fusion.refs_0_ = f32[4,8,64,768]{3,2,1,0:T(8,128)} fusion(f32[1,8,64,768]{3,2,1,0:T(8,128)} %bitcast.7, f32[1,8,64,768]{3,2,1,0:T(8,128)} %bitcast.6, f32[1,8,64,768]{3,2,1,0:T(8,128)} %bitcast.5, f32[1,8,64,768]{3,2,1,0:T(8,128)} %bitcast.17), kind=kLoop, calls=%fused_computation | loop fusion | flops 4718592 | bytes 12582912 | tf_op jit(solution)/shard_map/stack | solution.py:179
  197.2 2.8 pack.8
  201.8 2.7 collective-permute-start.15
  206.1 3.4 pack.10
  211.2 6.4 %collective-permute-done.15.refs_4_ = f32[8,64,128]{2,1,0:T(8,128)} collective-permute-done((f32[8,64,128]{2,1,0:T(8,128)}, f32[8,64,128]{2,1,0:T(8,128)}, u32[]{:S(2)}, u32[]{:S(2)}) %collective-permute-start.15) | collective-permute-done | bytes 262176 | tf_op jit(solution)/shard_map/ppermute | solution.py:24
  220.7 8.1 %collective-permute-done.21.refs_8_ = f32[16,64,128]{2,1,0:T(8,128)} collective-permute-done((f32[16,64,128]{2,1,0:T(8,128)}, f32[16,64,128]{2,1,0:T(8,128)}, u32[]{:S(2)}, u32[]{:S(2)}) %collective-permute-start.21) | collective-permute-done | bytes 524320 | tf_op jit(solution)/shard_map/ppermute | solution.py:24
  228.8 10.9 %collective-permute-done.22.refs_9_ = f32[16,64,128]{2,1,0:T(8,128)} collective-permute-done((f32[16,64,128]{2,1,0:T(8,128)}, f32[16,64,128]{2,1,0:T(8,128)}, u32[]{:S(2)}, u32[]{:S(2)}) %collective-permute-start.22) | collective-permute-done | bytes 524320 | tf_op jit(solution)/shard_map/ppermute | solution.py:24
  241.3 15.0 %product.2 = f32[2,8,64,128]{3,2,1,0:T(8,128)} custom-call(s32[4]{0:T(128)} %pad_add_fusion.7.meta, s32[768]{0:T(1024)} %get-tuple-element.43.pos, f32[4,8,64,768]{3,2,1,0:T(8,128)} %pad_maximum_fusion.1.refs_0_, f32[4,8,64,768]{3,2,1,0:T(8,128)} %collective-permute-done.12.refs_1_, f32[8,64,128]{2,1,0:T(8,128)} %get-tuple-element.21.refs_2_, ...), custom_call_target="tpu_custom_call" | custom-call | tf_op jit(solution)/shard_map/product/pallas_call | solution.py:115
  256.3 3.2 collective-permute-start.31
  259.7 11.7 %collective-permute-done.30.refs_0_ = f32[16,64,128]{2,1,0:T(8,128)} collective-permute-done((f32[16,64,128]{2,1,0:T(8,128)}, f32[16,64,128]{2,1,0:T(8,128)}, u32[]{:S(2)}, u32[]{:S(2)}) %collective-permute-start.30) | collective-permute-done | bytes 524320 | tf_op jit(solution)/shard_map/ppermute | solution.py:24
  272.7 3.4 pack.13
  276.1 4.2 %all-to-all-start.2 = ((f32[4,16,64,128]{3,2,1,0:T(8,128)}), f32[4,16,64,128]{3,2,1,0:T(8,128)S(1)}, u32[]{:S(2)}, u32[]{:S(2)}) async-start(f32[4,16,64,128]{3,2,1,0:T(8,128)} %pack.13), calls=%async_computation.2 | async-start | bytes 4194304 | tf_op jit(solution)/shard_map/all_to_all | solution.py:33
  280.4 3.2 collective-permute-start.33
  285.4 8.2 %collective-permute-done.33.refs_1_ = f32[16,64,128]{2,1,0:T(8,128)S(1)} collective-permute-done((f32[16,64,128]{2,1,0:T(8,128)S(1)}, f32[16,64,128]{2,1,0:T(8,128)S(1)}, u32[]{:S(2)}, u32[]{:S(2)}) %collective-permute-start.33) | collective-permute-done | bytes 524320 | tf_op jit(solution)/shard_map/ppermute | solution.py:24
  293.6 3.7 collective-permute-start.38
  298.3 8.0 %collective-permute-done.38.refs_1_ = f32[16,64,128]{2,1,0:T(8,128)S(1)} collective-permute-done((f32[16,64,128]{2,1,0:T(8,128)S(1)}, f32[16,64,128]{2,1,0:T(8,128)S(1)}, u32[]{:S(2)}, u32[]{:S(2)}) %collective-permute-start.38) | collective-permute-done | bytes 524320 | tf_op jit(solution)/shard_map/ppermute | solution.py:24
  306.3 4.2 %collective-permute-done.39.refs_2_ = f32[16,64,128]{2,1,0:T(8,128)} collective-permute-done((f32[16,64,128]{2,1,0:T(8,128)S(1)}, f32[16,64,128]{2,1,0:T(8,128)}, u32[]{:S(2)}, u32[]{:S(2)}) %collective-permute-start.39) | collective-permute-done | bytes 524320 | tf_op jit(solution)/shard_map/ppermute | solution.py:24
  310.6 3.9 pack.15
  315.8 5.2 %all-to-all-start.3 = ((f32[4,24,64,128]{3,2,1,0:T(8,128)}), f32[4,24,64,128]{3,2,1,0:T(8,128)S(1)}, u32[]{:S(2)}, u32[]{:S(2)}) async-start(f32[4,24,64,128]{3,2,1,0:T(8,128)} %pack.15), calls=%async_computation.3 | async-start | bytes 6291456 | tf_op jit(solution)/shard_map/all_to_all | solution.py:33
  321.0 2.8 pack.12
  323.9 2.0 collective-permute-start.27
  325.9 3.4 pack.14
  332.0 2.6 collective-permute-start.36
  335.5 29.9 %collective-permute-done.27.refs_3_ = f32[8,64,128]{2,1,0:T(8,128)S(1)} collective-permute-done((f32[8,64,128]{2,1,0:T(8,128)}, f32[8,64,128]{2,1,0:T(8,128)S(1)}, u32[]{:S(2)}, u32[]{:S(2)}) %collective-permute-start.27) | collective-permute-done | bytes 262176 | tf_op jit(solution)/shard_map/ppermute | solution.py:24
  366.3 22.9 %collective-permute-done.28.refs_4_ = f32[8,64,128]{2,1,0:T(8,128)S(1)} collective-permute-done((f32[8,64,128]{2,1,0:T(8,128)}, f32[8,64,128]{2,1,0:T(8,128)S(1)}, u32[]{:S(2)}, u32[]{:S(2)}) %collective-permute-start.28) | collective-permute-done | bytes 262176 | tf_op jit(solution)/shard_map/ppermute | solution.py:24
  392.5 15.0 %product.3 = f32[2,8,64,128]{3,2,1,0:T(8,128)} custom-call(s32[4]{0:T(128)} %pad_add_fusion.7.meta, s32[768]{0:T(1024)} %get-tuple-element.44.pos, f32[4,8,64,768]{3,2,1,0:T(8,128)} %pad_maximum_fusion.refs_0_, f32[4,8,64,768]{3,2,1,0:T(8,128)} %collective-permute-done.4.refs_1_, f32[8,64,128]{2,1,0:T(8,128)} %get-tuple-element.29.refs_2_, ...), custom_call_target="tpu_custom_call" | custom-call | tf_op jit(solution)/shard_map/product/pallas_call | solution.py:115
  (144 shorter events, 42.6 us)
Async XLA Ops:
  6.1 56.2 %copy-start.4 = (f32[8,64,768]{2,1,0:T(8,128)S(1)}, f32[8,64,768]{2,1,0:T(8,128)}, u32[]{:S(2)}) copy-start(f32[8,64,768]{2,1,0:T(8,128)} %turn.3) | copy-start | bytes 4718596
  6.1 36.3 %collective-permute-start.8 = (f32[8,64,768]{2,1,0:T(8,128)}, f32[8,64,768]{2,1,0:T(8,128)S(1)}, u32[]{:S(2)}, u32[]{:S(2)}) collective-permute-start(f32[8,64,768]{2,1,0:T(8,128)} %turn.3), channel_id=1, source_target_pairs={{0,1},{1,2},{2,3},{3,0},{4,5},{5,6},{6,7},{7,4},{8,9},{9,10},{10,1... | collective-permute-start | bytes 4718600 | tf_op jit(solution)/shard_map/ppermute | solution.py:28
  7.4 36.5 %collective-permute-start.9 = (f32[8,64,768]{2,1,0:T(8,128)}, f32[8,64,768]{2,1,0:T(8,128)S(1)}, u32[]{:S(2)}, u32[]{:S(2)}) collective-permute-start(f32[8,64,768]{2,1,0:T(8,128)} %turn.3), channel_id=1, source_target_pairs={{0,3},{1,0},{2,1},{3,2},{4,7},{5,4},{6,5},{7,6},{8,11},{9,8},{10,9... | collective-permute-start | bytes 4718600 | tf_op jit(solution)/shard_map/ppermute | solution.py:28
  42.5 18.5 %collective-permute-start.10 = (f32[4,64,768]{2,1,0:T(8,128)S(1)}, f32[4,64,768]{2,1,0:T(8,128)S(1)}, u32[]{:S(2)}, u32[]{:S(2)}) collective-permute-start(f32[4,64,768]{2,1,0:T(8,128)S(1)} %slice.78), channel_id=1, source_target_pairs={{0,1},{1,2},{2,3},{3,0},{4,5},{5,6},{6,7},{7,4},{8,9},{9,10},{10,1... | collective-permute-start | bytes 2359304 | tf_op jit(solution)/shard_map/ppermute | solution.py:28
  43.9 18.2 %collective-permute-start.11 = (f32[4,64,768]{2,1,0:T(8,128)S(1)}, f32[4,64,768]{2,1,0:T(8,128)S(1)}, u32[]{:S(2)}, u32[]{:S(2)}) collective-permute-start(f32[4,64,768]{2,1,0:T(8,128)S(1)} %slice.79), channel_id=1, source_target_pairs={{0,3},{1,0},{2,1},{3,2},{4,7},{5,4},{6,5},{7,6},{8,11},{9,8},{10,9... | collective-permute-start | bytes 2359304 | tf_op jit(solution)/shard_map/ppermute | solution.py:28
  62.3 35.8 %copy-start.23 = (s32[8,48]{1,0:T(8,128)S(1)}, s32[8,48]{1,0:T(8,128)}, u32[]{:S(2)}) copy-start(s32[8,48]{1,0:T(8,128)} %param.12) | copy-start | bytes 4612
  65.3 174.3 %collective-permute-start.12 = (f32[4,8,64,768]{3,2,1,0:T(8,128)}, f32[4,8,64,768]{3,2,1,0:T(8,128)}, u32[]{:S(2)}, u32[]{:S(2)}) collective-permute-start(f32[4,8,64,768]{3,2,1,0:T(8,128)} %pad_maximum_fusion.1.refs_0_), channel_id=1, source_target_pairs={{0,4},{4,0},{8,12},{12,8},{16,20},{20,16},{24,28},{28,24},{32,36},... | collective-permute-start | bytes 18874376 | tf_op jit(solution)/shard_map/ppermute | solution.py:24
  65.4 10.7 %collective-permute-start.13 = (f32[512,128]{1,0:T(8,128)S(1)}, f32[512,128]{1,0:T(8,128)S(1)}, u32[]{:S(2)}, u32[]{:S(2)}) collective-permute-start(f32[512,128]{1,0:T(8,128)S(1)} %get-tuple-element.40), channel_id=1, source_target_pairs={{0,4},{4,0},{8,12},{12,8},{16,20},{20,16},{24,28},{28,24},{32,36},... | collective-permute-start | bytes 786440 | tf_op jit(solution)/shard_map/ppermute | solution.py:24
  76.1 36.8 %copy-start.5 = (f32[1024,128]{1,0:T(8,128)}, f32[1024,128]{1,0:T(8,128)S(1)}, u32[]{:S(2)}) copy-start(f32[1024,128]{1,0:T(8,128)S(1)} %pad_maximum_fusion.2) | copy-start | bytes 1572868
  76.1 18.2 %collective-permute-start.17 = (f32[16,64,128]{2,1,0:T(8,128)S(1)}, f32[16,64,128]{2,1,0:T(8,128)S(1)}, u32[]{:S(2)}, u32[]{:S(2)}) collective-permute-start(f32[16,64,128]{2,1,0:T(8,128)S(1)} %bitcast.24), channel_id=1, source_target_pairs={{0,32},{4,36},{8,40},{12,44},{16,48},{20,52},{24,56},{28,60},{32,6... | collective-permute-start | bytes 1572872 | tf_op jit(solution)/shard_map/ppermute | solution.py:24
  78.1 16.7 %collective-permute-start.18 = (f32[16,64,128]{2,1,0:T(8,128)S(1)}, f32[16,64,128]{2,1,0:T(8,128)}, u32[]{:S(2)}, u32[]{:S(2)}) collective-permute-start(f32[16,64,128]{2,1,0:T(8,128)S(1)} %bitcast.25), channel_id=1, source_target_pairs={{0,224},{4,228},{8,232},{12,236},{16,240},{20,244},{24,248},{28,25... | collective-permute-start | bytes 1572872 | tf_op jit(solution)/shard_map/ppermute | solution.py:24
  94.3 14.6 %collective-permute-start.19 = (f32[16,64,128]{2,1,0:T(8,128)S(1)}, f32[16,64,128]{2,1,0:T(8,128)S(1)}, u32[]{:S(2)}, u32[]{:S(2)}) collective-permute-start(f32[16,64,128]{2,1,0:T(8,128)S(1)} %collective-permute-done.17.refs_0_), channel_id=1, source_target_pairs={{0,32},{4,36},{8,40},{12,44},{16,48},{20,52},{24,56},{28,60},{32,6... | collective-permute-start | bytes 1572872 | tf_op jit(solution)/shard_map/ppermute | solution.py:24
  94.8 31.4 %collective-permute-start.20 = (f32[16,64,128]{2,1,0:T(8,128)}, f32[16,64,128]{2,1,0:T(8,128)S(1)}, u32[]{:S(2)}, u32[]{:S(2)}) collective-permute-start(f32[16,64,128]{2,1,0:T(8,128)} %collective-permute-done.18.refs_1_), channel_id=1, source_target_pairs={{0,224},{4,228},{8,232},{12,236},{16,240},{20,244},{24,248},{28,25... | collective-permute-start | bytes 1572872 | tf_op jit(solution)/shard_map/ppermute | solution.py:24
  98.1 1.3 collective-permute-start
  99.4 4.1 %collective-permute-start.5 = (s32[4,128]{1,0:T(4,128)S(1)}, s32[4,128]{1,0:T(4,128)S(1)}, u32[]{:S(2)}, u32[]{:S(2)}) collective-permute-start(s32[4,128]{1,0:T(4,128)S(1)} %pad_add_fusion.6), channel_id=1, source_target_pairs={{0,24},{4,28},{8,0},{12,4},{16,8},{20,12},{24,16},{28,20},{32,56},... | collective-permute-start | bytes 6152 | tf_op jit(solution)/shard_map/ppermute | solution.py:24
  102.2 5.1 %collective-permute-start.6 = (s32[4,128]{1,0:T(4,128)S(1)}, s32[4,128]{1,0:T(4,128)S(1)}, u32[]{:S(2)}, u32[]{:S(2)}) collective-permute-start(s32[4,128]{1,0:T(4,128)S(1)} %pad_add_fusion.6), channel_id=1, source_target_pairs={{0,16},{4,20},{8,24},{12,28},{16,0},{20,4},{24,8},{28,12},{32,48},... | collective-permute-start | bytes 6152 | tf_op jit(solution)/shard_map/ppermute | solution.py:24
  103.5 5.0 %collective-permute-start.7 = (s32[4,128]{1,0:T(4,128)S(1)}, s32[4,128]{1,0:T(4,128)S(1)}, u32[]{:S(2)}, u32[]{:S(2)}) collective-permute-start(s32[4,128]{1,0:T(4,128)S(1)} %pad_add_fusion.6), channel_id=1, source_target_pairs={{0,8},{4,12},{8,16},{12,20},{16,24},{20,28},{24,0},{28,4},{32,40},... | collective-permute-start | bytes 6152 | tf_op jit(solution)/shard_map/ppermute | solution.py:24
  108.9 19.6 %collective-permute-start.24 = (f32[16,64,128]{2,1,0:T(8,128)S(1)}, f32[16,64,128]{2,1,0:T(8,128)}, u32[]{:S(2)}, u32[]{:S(2)}) collective-permute-start(f32[16,64,128]{2,1,0:T(8,128)S(1)} %collective-permute-done.19.refs_0_), channel_id=1, source_target_pairs={{0,32},{4,36},{8,40},{12,44},{16,48},{20,52},{24,56},{28,60},{32,6... | collective-permute-start | bytes 1572872 | tf_op jit(solution)/shard_map/ppermute | solution.py:24
  112.9 44.2 %all-to-all-start = ((f32[4,16,64,128]{3,2,1,0:T(8,128)}), f32[4,16,64,128]{3,2,1,0:T(8,128)S(1)}, u32[]{:S(2)}, u32[]{:S(2)}) async-start(f32[4,16,64,128]{3,2,1,0:T(8,128)} %pack.9), calls=%async_computation | async-start | bytes 4194304 | tf_op jit(solution)/shard_map/all_to_all | solution.py:33
  123.3 39.3 %collective-permute-start.1 = (f32[8,64,768]{2,1,0:T(8,128)}, f32[8,64,768]{2,1,0:T(8,128)}, u32[]{:S(2)}, u32[]{:S(2)}) collective-permute-start(f32[8,64,768]{2,1,0:T(8,128)} %turn.2), channel_id=1, source_target_pairs={{0,1},{1,2},{2,3},{3,0},{4,5},{5,6},{6,7},{7,4},{8,9},{9,10},{10,1... | collective-permute-start | bytes 4718600 | tf_op jit(solution)/shard_map/ppermute | solution.py:28
  126.2 37.6 %collective-permute-start.2 = (f32[8,64,768]{2,1,0:T(8,128)}, f32[8,64,768]{2,1,0:T(8,128)}, u32[]{:S(2)}, u32[]{:S(2)}) collective-permute-start(f32[8,64,768]{2,1,0:T(8,128)} %turn.2), channel_id=1, source_target_pairs={{0,3},{1,0},{2,1},{3,2},{4,7},{5,4},{6,5},{7,6},{8,11},{9,8},{10,9... | collective-permute-start | bytes 4718600 | tf_op jit(solution)/shard_map/ppermute | solution.py:28
  126.2 66.3 %collective-permute-start.3 = (f32[8,64,768]{2,1,0:T(8,128)}, f32[8,64,768]{2,1,0:T(8,128)}, u32[]{:S(2)}, u32[]{:S(2)}) collective-permute-start(f32[8,64,768]{2,1,0:T(8,128)} %turn.2), channel_id=1, source_target_pairs={{0,2},{1,3},{2,0},{3,1},{4,6},{5,7},{6,4},{7,5},{8,10},{9,11},{10,... | collective-permute-start | bytes 4718600 | tf_op jit(solution)/shard_map/ppermute | solution.py:28
  128.4 12.0 %collective-permute-start.25 = (f32[16,64,128]{2,1,0:T(8,128)S(1)}, f32[16,64,128]{2,1,0:T(8,128)S(1)}, u32[]{:S(2)}, u32[]{:S(2)}) collective-permute-start(f32[16,64,128]{2,1,0:T(8,128)S(1)} %collective-permute-done.20.refs_1_), channel_id=1, source_target_pairs={{0,224},{4,228},{8,232},{12,236},{16,240},{20,244},{24,248},{28,25... | collective-permute-start | bytes 1572872 | tf_op jit(solution)/shard_map/ppermute | solution.py:24
  140.4 12.7 %collective-permute-start.26 = (f32[16,64,128]{2,1,0:T(8,128)}, f32[16,64,128]{2,1,0:T(8,128)}, u32[]{:S(2)}, u32[]{:S(2)}) collective-permute-start(f32[16,64,128]{2,1,0:T(8,128)} %collective-permute-done.24.refs_0_), channel_id=1, source_target_pairs={{0,32},{4,36},{8,40},{12,44},{16,48},{20,52},{24,56},{28,60},{32,6... | collective-permute-start | bytes 1572872 | tf_op jit(solution)/shard_map/ppermute | solution.py:24
  158.4 81.2 %all-to-all-start.1 = ((f32[4,24,64,128]{3,2,1,0:T(8,128)}), f32[4,24,64,128]{3,2,1,0:T(8,128)S(1)}, u32[]{:S(2)}, u32[]{:S(2)}) async-start(f32[4,24,64,128]{3,2,1,0:T(8,128)} %pack.11), calls=%async_computation.1 | async-start | bytes 6291456 | tf_op jit(solution)/shard_map/all_to_all | solution.py:33
  197.2 137.4 %collective-permute-start.4 = (f32[4,8,64,768]{3,2,1,0:T(8,128)}, f32[4,8,64,768]{3,2,1,0:T(8,128)}, u32[]{:S(2)}, u32[]{:S(2)}) collective-permute-start(f32[4,8,64,768]{3,2,1,0:T(8,128)} %pad_maximum_fusion.refs_0_), channel_id=1, source_target_pairs={{0,4},{4,0},{8,12},{12,8},{16,20},{20,16},{24,28},{28,24},{32,36},... | collective-permute-start | bytes 18874376 | tf_op jit(solution)/shard_map/ppermute | solution.py:24
  200.1 10.1 %collective-permute-start.14 = (f32[8,64,128]{2,1,0:T(8,128)}, f32[8,64,128]{2,1,0:T(8,128)S(1)}, u32[]{:S(2)}, u32[]{:S(2)}) collective-permute-start(f32[8,64,128]{2,1,0:T(8,128)} %get-tuple-element.22), channel_id=1, source_target_pairs={{0,8},{4,12},{8,16},{12,20},{16,24},{20,28},{24,0},{28,4},{32,40},... | collective-permute-start | bytes 786440 | tf_op jit(solution)/shard_map/ppermute | solution.py:24
  201.8 15.8 %collective-permute-start.15 = (f32[8,64,128]{2,1,0:T(8,128)}, f32[8,64,128]{2,1,0:T(8,128)}, u32[]{:S(2)}, u32[]{:S(2)}) collective-permute-start(f32[8,64,128]{2,1,0:T(8,128)} %get-tuple-element.23), channel_id=1, source_target_pairs={{0,16},{4,20},{8,24},{12,28},{16,0},{20,4},{24,8},{28,12},{32,48},... | collective-permute-start | bytes 786440 | tf_op jit(solution)/shard_map/ppermute | solution.py:24
  204.5 14.0 %collective-permute-start.16 = (f32[8,64,128]{2,1,0:T(8,128)}, f32[8,64,128]{2,1,0:T(8,128)}, u32[]{:S(2)}, u32[]{:S(2)}) collective-permute-start(f32[8,64,128]{2,1,0:T(8,128)} %get-tuple-element.24), channel_id=1, source_target_pairs={{0,24},{4,28},{8,0},{12,4},{16,8},{20,12},{24,16},{28,20},{32,56},... | collective-permute-start | bytes 786440 | tf_op jit(solution)/shard_map/ppermute | solution.py:24
  210.2 18.6 %collective-permute-start.21 = (f32[16,64,128]{2,1,0:T(8,128)}, f32[16,64,128]{2,1,0:T(8,128)}, u32[]{:S(2)}, u32[]{:S(2)}) collective-permute-start(f32[16,64,128]{2,1,0:T(8,128)} %get-tuple-element.26), channel_id=1, source_target_pairs={{0,8},{4,12},{8,16},{12,20},{16,24},{20,28},{24,0},{28,4},{32,40},... | collective-permute-start | bytes 1572872 | tf_op jit(solution)/shard_map/ppermute | solution.py:24
  217.6 22.0 %collective-permute-start.22 = (f32[16,64,128]{2,1,0:T(8,128)}, f32[16,64,128]{2,1,0:T(8,128)}, u32[]{:S(2)}, u32[]{:S(2)}) collective-permute-start(f32[16,64,128]{2,1,0:T(8,128)} %get-tuple-element.27), channel_id=1, source_target_pairs={{0,16},{4,20},{8,24},{12,28},{16,0},{20,4},{24,8},{28,12},{32,48},... | collective-permute-start | bytes 1572872 | tf_op jit(solution)/shard_map/ppermute | solution.py:24
  218.5 21.1 %collective-permute-start.23 = (f32[16,64,128]{2,1,0:T(8,128)}, f32[16,64,128]{2,1,0:T(8,128)}, u32[]{:S(2)}, u32[]{:S(2)}) collective-permute-start(f32[16,64,128]{2,1,0:T(8,128)} %get-tuple-element.28), channel_id=1, source_target_pairs={{0,24},{4,28},{8,0},{12,4},{16,8},{20,12},{24,16},{28,20},{32,56},... | collective-permute-start | bytes 1572872 | tf_op jit(solution)/shard_map/ppermute | solution.py:24
  256.2 15.1 %collective-permute-start.30 = (f32[16,64,128]{2,1,0:T(8,128)}, f32[16,64,128]{2,1,0:T(8,128)}, u32[]{:S(2)}, u32[]{:S(2)}) collective-permute-start(f32[16,64,128]{2,1,0:T(8,128)} %bitcast.21), channel_id=1, source_target_pairs={{0,32},{4,36},{8,40},{12,44},{16,48},{20,52},{24,56},{28,60},{32,6... | collective-permute-start | bytes 1572872 | tf_op jit(solution)/shard_map/ppermute | solution.py:24
  256.3 15.6 %collective-permute-start.31 = (f32[16,64,128]{2,1,0:T(8,128)}, f32[16,64,128]{2,1,0:T(8,128)S(1)}, u32[]{:S(2)}, u32[]{:S(2)}) collective-permute-start(f32[16,64,128]{2,1,0:T(8,128)} %bitcast.22), channel_id=1, source_target_pairs={{0,224},{4,228},{8,232},{12,236},{16,240},{20,244},{24,248},{28,25... | collective-permute-start | bytes 1572872 | tf_op jit(solution)/shard_map/ppermute | solution.py:24
  271.3 14.0 %collective-permute-start.32 = (f32[16,64,128]{2,1,0:T(8,128)}, f32[16,64,128]{2,1,0:T(8,128)S(1)}, u32[]{:S(2)}, u32[]{:S(2)}) collective-permute-start(f32[16,64,128]{2,1,0:T(8,128)} %collective-permute-done.30.refs_0_), channel_id=1, source_target_pairs={{0,32},{4,36},{8,40},{12,44},{16,48},{20,52},{24,56},{28,60},{32,6... | collective-permute-start | bytes 1572872 | tf_op jit(solution)/shard_map/ppermute | solution.py:24
  276.1 38.4 %all-to-all-start.2 = ((f32[4,16,64,128]{3,2,1,0:T(8,128)}), f32[4,16,64,128]{3,2,1,0:T(8,128)S(1)}, u32[]{:S(2)}, u32[]{:S(2)}) async-start(f32[4,16,64,128]{3,2,1,0:T(8,128)} %pack.13), calls=%async_computation.2 | async-start | bytes 4194304 | tf_op jit(solution)/shard_map/all_to_all | solution.py:33
  280.4 13.2 %collective-permute-start.33 = (f32[16,64,128]{2,1,0:T(8,128)S(1)}, f32[16,64,128]{2,1,0:T(8,128)S(1)}, u32[]{:S(2)}, u32[]{:S(2)}) collective-permute-start(f32[16,64,128]{2,1,0:T(8,128)S(1)} %copy-done.15), channel_id=1, source_target_pairs={{0,224},{4,228},{8,232},{12,236},{16,240},{20,244},{24,248},{28,25... | collective-permute-start | bytes 1572872 | tf_op jit(solution)/shard_map/ppermute | solution.py:24
  285.4 13.0 %collective-permute-start.37 = (f32[16,64,128]{2,1,0:T(8,128)S(1)}, f32[16,64,128]{2,1,0:T(8,128)S(1)}, u32[]{:S(2)}, u32[]{:S(2)}) collective-permute-start(f32[16,64,128]{2,1,0:T(8,128)S(1)} %collective-permute-done.32.refs_0_), channel_id=1, source_target_pairs={{0,32},{4,36},{8,40},{12,44},{16,48},{20,52},{24,56},{28,60},{32,6... | collective-permute-start | bytes 1572872 | tf_op jit(solution)/shard_map/ppermute | solution.py:24
  293.6 12.8 %collective-permute-start.38 = (f32[16,64,128]{2,1,0:T(8,128)S(1)}, f32[16,64,128]{2,1,0:T(8,128)S(1)}, u32[]{:S(2)}, u32[]{:S(2)}) collective-permute-start(f32[16,64,128]{2,1,0:T(8,128)S(1)} %collective-permute-done.33.refs_1_), channel_id=1, source_target_pairs={{0,224},{4,228},{8,232},{12,236},{16,240},{20,244},{24,248},{28,25... | collective-permute-start | bytes 1572872 | tf_op jit(solution)/shard_map/ppermute | solution.py:24
  298.3 12.2 %collective-permute-start.39 = (f32[16,64,128]{2,1,0:T(8,128)S(1)}, f32[16,64,128]{2,1,0:T(8,128)}, u32[]{:S(2)}, u32[]{:S(2)}) collective-permute-start(f32[16,64,128]{2,1,0:T(8,128)S(1)} %collective-permute-done.37.refs_0_), channel_id=1, source_target_pairs={{0,32},{4,36},{8,40},{12,44},{16,48},{20,52},{24,56},{28,60},{32,6... | collective-permute-start | bytes 1572872 | tf_op jit(solution)/shard_map/ppermute | solution.py:24
  315.8 75.1 %all-to-all-start.3 = ((f32[4,24,64,128]{3,2,1,0:T(8,128)}), f32[4,24,64,128]{3,2,1,0:T(8,128)S(1)}, u32[]{:S(2)}, u32[]{:S(2)}) async-start(f32[4,24,64,128]{3,2,1,0:T(8,128)} %pack.15), calls=%async_computation.3 | async-start | bytes 6291456 | tf_op jit(solution)/shard_map/all_to_all | solution.py:33
  323.9 41.5 %collective-permute-start.27 = (f32[8,64,128]{2,1,0:T(8,128)}, f32[8,64,128]{2,1,0:T(8,128)S(1)}, u32[]{:S(2)}, u32[]{:S(2)}) collective-permute-start(f32[8,64,128]{2,1,0:T(8,128)} %get-tuple-element.30), channel_id=1, source_target_pairs={{0,8},{4,12},{8,16},{12,20},{16,24},{20,28},{24,0},{28,4},{32,40},... | collective-permute-start | bytes 786440 | tf_op jit(solution)/shard_map/ppermute | solution.py:24
  329.3 59.8 %collective-permute-start.34 = (f32[16,64,128]{2,1,0:T(8,128)}, f32[16,64,128]{2,1,0:T(8,128)S(1)}, u32[]{:S(2)}, u32[]{:S(2)}) collective-permute-start(f32[16,64,128]{2,1,0:T(8,128)} %get-tuple-element.34), channel_id=1, source_target_pairs={{0,8},{4,12},{8,16},{12,20},{16,24},{20,28},{24,0},{28,4},{32,40},... | collective-permute-start | bytes 1572872 | tf_op jit(solution)/shard_map/ppermute | solution.py:24
  330.8 58.4 %collective-permute-start.35 = (f32[16,64,128]{2,1,0:T(8,128)}, f32[16,64,128]{2,1,0:T(8,128)S(1)}, u32[]{:S(2)}, u32[]{:S(2)}) collective-permute-start(f32[16,64,128]{2,1,0:T(8,128)} %get-tuple-element.35), channel_id=1, source_target_pairs={{0,16},{4,20},{8,24},{12,28},{16,0},{20,4},{24,8},{28,12},{32,48},... | collective-permute-start | bytes 1572872 | tf_op jit(solution)/shard_map/ppermute | solution.py:24
  332.0 58.9 %collective-permute-start.36 = (f32[16,64,128]{2,1,0:T(8,128)}, f32[16,64,128]{2,1,0:T(8,128)}, u32[]{:S(2)}, u32[]{:S(2)}) collective-permute-start(f32[16,64,128]{2,1,0:T(8,128)} %get-tuple-element.36), channel_id=1, source_target_pairs={{0,24},{4,28},{8,0},{12,4},{16,8},{20,12},{24,16},{28,20},{32,56},... | collective-permute-start | bytes 1572872 | tf_op jit(solution)/shard_map/ppermute | solution.py:24
  334.6 54.5 %collective-permute-start.28 = (f32[8,64,128]{2,1,0:T(8,128)}, f32[8,64,128]{2,1,0:T(8,128)S(1)}, u32[]{:S(2)}, u32[]{:S(2)}) collective-permute-start(f32[8,64,128]{2,1,0:T(8,128)} %get-tuple-element.31), channel_id=1, source_target_pairs={{0,16},{4,20},{8,24},{12,28},{16,0},{20,4},{24,8},{28,12},{32,48},... | collective-permute-start | bytes 786440 | tf_op jit(solution)/shard_map/ppermute | solution.py:24
  365.4 23.8 %collective-permute-start.29 = (f32[8,64,128]{2,1,0:T(8,128)}, f32[8,64,128]{2,1,0:T(8,128)S(1)}, u32[]{:S(2)}, u32[]{:S(2)}) collective-permute-start(f32[8,64,128]{2,1,0:T(8,128)} %get-tuple-element.32), channel_id=1, source_target_pairs={{0,24},{4,28},{8,0},{12,4},{16,8},{20,12},{24,16},{28,20},{32,56},... | collective-permute-start | bytes 786440 | tf_op jit(solution)/shard_map/ppermute | solution.py:24
  408.6 1.6 collective-permute-start.40
  (24 other events, 281.2 us)
where the time goes:
time: 417 us; the launch traced here: 411 us
  waiting for transfers between devices  246 us (59%)
  starting transfers between devices  73.7 us (18%)
  Pallas kernels  69.2 us (17%)
  other arithmetic  11.3 us (3%)
  local copies, waits for them, and re-layouts  10.6 us (3%)
    ppermute x34, waiting for transfers between devices, rows_shift(): return lax.ppermute(array, 'rows', pairs)  164 us
    ppermute x7, waiting for transfers between devices, cols_shift(): return lax.ppermute(array, 'cols', [(y, (y + dy) % NY) for y in range(NY)])  81.6 us
    ppermute x34, starting transfers between devices, rows_shift(): return lax.ppermute(array, 'rows', pairs)  46.4 us
    pallas_call x2, Pallas kernels, product(): pl.pallas_call(product_kernel, out_shape=jax.ShapeDtypeStruct((2, 8, B, H...  29.9 us
    pallas_call x8, Pallas kernels, pack(): pl.pallas_call(functools.partial(pack_kernel, offsets, whole), out_shape=...  27.1 us
    all_to_all x4, starting transfers between devices, x_exchange(): lax.all_to_all(array, 'rows', 0, 0, axis_index_groups=groups, tiled=True)  18 us
    pallas_call x2, Pallas kernels, gather_blocks(): pl.pallas_call(turn_kernel, out_shape=jax.ShapeDtypeStruct((8, B, 768), j...  12.2 us
    ppermute x7, starting transfers between devices, cols_shift(): return lax.ppermute(array, 'cols', [(y, (y + dy) % NY) for y in range(NY)])  9.32 us
  transfers between devices with their start and end apart: 45, of which 27 were waited for; matrix products, arithmetic and copies ran while one was open for 2% of the time, Pallas kernels for 12%

commit v1 on v0

--- a/solution.py
+++ b/solution.py
@@ -11,6 +11,7 @@
 B, HALF = 64, 128
 GROUPS = ((0,), (7, 1), (6, 2), (5, 3, 4))
 
+STARTS = (0, 1, 3, 5)
 WHOLE = (False, True, False, True)
 
 
@@ -77,10 +78,8 @@
             for s in range(NX):
                 xp = (x - s) & 3
                 part = block.at[xp] if WHOLE[g] else next(arrived)
-                for n, off in enumerate(offsets):
-                    pltpu.make_async_copy(
-                        part.at[pl.ds(n * 8, 8)], slabs.at[pl.ds((xp * NZ + off) * 8, 8)], sems.at[xp]
-                    ).start()
+                n = len(offsets) * 8
+                pltpu.make_async_copy(part, slabs.at[pl.ds(xp * 64 + STARTS[g] * 8, n)], sems.at[xp]).start()
         for xp in range(NX):
             part = slabs.at[pl.ds(xp * 64, 64)]
             pltpu.make_async_copy(part, part, sems.at[xp]).wait()
@@ -184,7 +183,9 @@
     owner, f = slots // 2, slots % 2
     zp, xp, cp = owner // 8, (owner // 2) % 4, owner % 2
     l = lax.broadcasted_iota(jnp.int32, slots.shape, 0) // 8
-    return ((xp * NZ + (zp - z) % NZ) * 8 + (cp ^ c) * 4 + l * 2 + f).reshape(-1)
+    off = (zp - z) % NZ
+    order = jnp.where(off < 4, 2 * off, jnp.where(off == 4, 7, 15 - 2 * off))
+    return ((xp * NZ + order) * 8 + (cp ^ c) * 4 + l * 2 + f).reshape(-1)
 
 
 def body(h_blocks, p_blocks, h_fetch, p_fetch, h_slot, p_slot, p_panel):

time: 417 us -> 417 us (level)
  no operation moved by 1% of the time
where the time goes in v1:
time: 417 us; the launch traced here: 411 us
  waiting for transfers between devices  246 us (59%)
  starting transfers between devices  73.9 us (18%)
  Pallas kernels  69.3 us (17%)
  other arithmetic  11.3 us (3%)
  local copies, waits for them, and re-layouts  10.6 us (3%)
    ppermute x34, waiting for transfers between devices, rows_shift(): return lax.ppermute(array, 'rows', pairs)  164 us
    ppermute x7, waiting for transfers between devices, cols_shift(): return lax.ppermute(array, 'cols', [(y, (y + dy) % NY) for y in range(NY)])  81.6 us
    ppermute x34, starting transfers between devices, rows_shift(): return lax.ppermute(array, 'rows', pairs)  46.4 us
    pallas_call x2, Pallas kernels, product(): pl.pallas_call(product_kernel, out_shape=jax.ShapeDtypeStruct((2, 8, B, H...  30 us
    pallas_call x8, Pallas kernels, pack(): pl.pallas_call(functools.partial(pack_kernel, offsets, whole), out_shape=...  27.1 us
    all_to_all x4, starting transfers between devices, x_exchange(): lax.all_to_all(array, 'rows', 0, 0, axis_index_groups=groups, tiled=True)  18.2 us
    pallas_call x2, Pallas kernels, gather_blocks(): pl.pallas_call(turn_kernel, out_shape=jax.ShapeDtypeStruct((8, B, 768), j...  12.2 us
    ppermute x7, starting transfers between devices, cols_shift(): return lax.ppermute(array, 'cols', [(y, (y + dy) % NY) for y in range(NY)])  9.32 us
  transfers between devices with their start and end apart: 45, of which 27 were waited for; matrix products, arithmetic and copies ran while one was open for 2% of the time, Pallas kernels for 12%

profile of v1, /device:TPU:16, one launch (start us, length us, event | category | flops | bytes accessed | tf_op | source)
XLA Modules:
  0.0 411.1 jit_solution(7004519662870318385)
XLA Ops:
  0.0 6.1 %turn.3 = f32[8,64,768]{2,1,0:T(8,128)} custom-call(f32[8,12,64,64]{3,2,1,0:T(8,128)} %blocks.3), custom_call_target="tpu_custom_call" | custom-call | tf_op jit(solution)/shard_map/turn/pallas_call | solution.py:158
  8.1 34.3 %collective-permute-done.8 = f32[8,64,768]{2,1,0:T(8,128)S(1)} collective-permute-done((f32[8,64,768]{2,1,0:T(8,128)}, f32[8,64,768]{2,1,0:T(8,128)S(1)}, u32[]{:S(2)}, u32[]{:S(2)}) %collective-permute-start.8) | collective-permute-done | bytes 1572896 | tf_op jit(solution)/shard_map/ppermute | solution.py:29
  44.8 16.3 %collective-permute-done.10 = f32[4,64,768]{2,1,0:T(8,128)S(1)} collective-permute-done((f32[4,64,768]{2,1,0:T(8,128)S(1)}, f32[4,64,768]{2,1,0:T(8,128)S(1)}, u32[]{:S(2)}, u32[]{:S(2)}) %collective-permute-start.10) | collective-permute-done | bytes 786464 | tf_op jit(solution)/shard_map/ppermute | solution.py:29
  62.4 3.0 pad_maximum_fusion.1.refs_0_
  66.0 10.1 %collective-permute-done.13 = f32[512,128]{1,0:T(8,128)S(1)} collective-permute-done((f32[512,128]{1,0:T(8,128)S(1)}, f32[512,128]{1,0:T(8,128)S(1)}, u32[]{:S(2)}, u32[]{:S(2)}) %collective-permute-start.13) | collective-permute-done | bytes 262176 | tf_op jit(solution)/shard_map/ppermute | solution.py:25
  76.1 2.0 collective-permute-start.17
  78.1 4.0 collective-permute-start.18
  82.1 12.1 %collective-permute-done.17.refs_0_ = f32[16,64,128]{2,1,0:T(8,128)S(1)} collective-permute-done((f32[16,64,128]{2,1,0:T(8,128)S(1)}, f32[16,64,128]{2,1,0:T(8,128)S(1)}, u32[]{:S(2)}, u32[]{:S(2)}) %collective-permute-start.17) | collective-permute-done | bytes 524320 | tf_op jit(solution)/shard_map/ppermute | solution.py:25
  94.8 3.3 collective-permute-start.20
  99.4 2.8 collective-permute-start.5
  105.2 2.2 collective-permute-done.6
  109.5 3.4 pack.9
  112.9 4.3 %all-to-all-start = ((f32[4,16,64,128]{3,2,1,0:T(8,128)}), f32[4,16,64,128]{3,2,1,0:T(8,128)S(1)}, u32[]{:S(2)}, u32[]{:S(2)}) async-start(f32[4,16,64,128]{3,2,1,0:T(8,128)} %pack.9), calls=%async_computation | async-start | bytes 4194304 | tf_op jit(solution)/shard_map/all_to_all | solution.py:34
  117.2 6.1 %turn.2 = f32[8,64,768]{2,1,0:T(8,128)} custom-call(f32[8,12,64,64]{3,2,1,0:T(8,128)} %blocks.2), custom_call_target="tpu_custom_call" | custom-call | tf_op jit(solution)/shard_map/turn/pallas_call | solution.py:158
  123.3 2.9 collective-permute-start.1
  126.2 2.2 collective-permute-start.3
  128.4 3.2 collective-permute-start.25
  131.6 8.8 %collective-permute-done.25.refs_1_ = f32[16,64,128]{2,1,0:T(8,128)S(1)} collective-permute-done((f32[16,64,128]{2,1,0:T(8,128)S(1)}, f32[16,64,128]{2,1,0:T(8,128)S(1)}, u32[]{:S(2)}, u32[]{:S(2)}) %collective-permute-start.25) | collective-permute-done | bytes 524320 | tf_op jit(solution)/shard_map/ppermute | solution.py:25
  140.4 12.7 %collective-permute-done.26.refs_2_ = f32[16,64,128]{2,1,0:T(8,128)} collective-permute-done((f32[16,64,128]{2,1,0:T(8,128)}, f32[16,64,128]{2,1,0:T(8,128)}, u32[]{:S(2)}, u32[]{:S(2)}) %collective-permute-start.26) | collective-permute-done | bytes 524320 | tf_op jit(solution)/shard_map/ppermute | solution.py:25
  153.1 3.9 pack.11
  158.4 4.2 %all-to-all-start.1 = ((f32[4,24,64,128]{3,2,1,0:T(8,128)}), f32[4,24,64,128]{3,2,1,0:T(8,128)S(1)}, u32[]{:S(2)}, u32[]{:S(2)}) async-start(f32[4,24,64,128]{3,2,1,0:T(8,128)} %pack.11), calls=%async_computation.1 | async-start | bytes 6291456 | tf_op jit(solution)/shard_map/all_to_all | solution.py:34
  163.8 28.7 %collective-permute-done.3 = f32[8,64,768]{2,1,0:T(8,128)} collective-permute-done((f32[8,64,768]{2,1,0:T(8,128)}, f32[8,64,768]{2,1,0:T(8,128)}, u32[]{:S(2)}, u32[]{:S(2)}) %collective-permute-start.3) | collective-permute-done | bytes 1572896 | tf_op jit(solution)/shard_map/ppermute | solution.py:29
  192.5 4.7 %pad_maximum_fusion.refs_0_ = f32[4,8,64,768]{3,2,1,0:T(8,128)} fusion(f32[1,8,64,768]{3,2,1,0:T(8,128)} %bitcast.7, f32[1,8,64,768]{3,2,1,0:T(8,128)} %bitcast.6, f32[1,8,64,768]{3,2,1,0:T(8,128)} %bitcast.5, f32[1,8,64,768]{3,2,1,0:T(8,128)} %bitcast.17), kind=kLoop, calls=%fused_computation | loop fusion | flops 4718592 | bytes 12582912 | tf_op jit(solution)/shard_map/stack | solution.py:178
  197.2 2.8 pack.8
  201.8 2.7 collective-permute-start.15
  206.1 3.4 pack.10
  211.2 6.4 %collective-permute-done.15.refs_4_ = f32[8,64,128]{2,1,0:T(8,128)} collective-permute-done((f32[8,64,128]{2,1,0:T(8,128)}, f32[8,64,128]{2,1,0:T(8,128)}, u32[]{:S(2)}, u32[]{:S(2)}) %collective-permute-start.15) | collective-permute-done | bytes 262176 | tf_op jit(solution)/shard_map/ppermute | solution.py:25
  220.7 8.1 %collective-permute-done.21.refs_8_ = f32[16,64,128]{2,1,0:T(8,128)} collective-permute-done((f32[16,64,128]{2,1,0:T(8,128)}, f32[16,64,128]{2,1,0:T(8,128)}, u32[]{:S(2)}, u32[]{:S(2)}) %collective-permute-start.21) | collective-permute-done | bytes 524320 | tf_op jit(solution)/shard_map/ppermute | solution.py:25
  228.8 10.9 %collective-permute-done.22.refs_9_ = f32[16,64,128]{2,1,0:T(8,128)} collective-permute-done((f32[16,64,128]{2,1,0:T(8,128)}, f32[16,64,128]{2,1,0:T(8,128)}, u32[]{:S(2)}, u32[]{:S(2)}) %collective-permute-start.22) | collective-permute-done | bytes 524320 | tf_op jit(solution)/shard_map/ppermute | solution.py:25
  241.3 15.0 %product.2 = f32[2,8,64,128]{3,2,1,0:T(8,128)} custom-call(s32[4]{0:T(128)} %pad_add_fusion.7.meta, s32[768]{0:T(1024)} %get-tuple-element.43.pos, f32[4,8,64,768]{3,2,1,0:T(8,128)} %pad_maximum_fusion.1.refs_0_, f32[4,8,64,768]{3,2,1,0:T(8,128)} %collective-permute-done.12.refs_1_, f32[8,64,128]{2,1,0:T(8,128)} %get-tuple-element.21.refs_2_, ...), custom_call_target="tpu_custom_call" | custom-call | tf_op jit(solution)/shard_map/product/pallas_call | solution.py:114
  256.4 3.2 collective-permute-start.31
  259.7 11.7 %collective-permute-done.30.refs_0_ = f32[16,64,128]{2,1,0:T(8,128)} collective-permute-done((f32[16,64,128]{2,1,0:T(8,128)}, f32[16,64,128]{2,1,0:T(8,128)}, u32[]{:S(2)}, u32[]{:S(2)}) %collective-permute-start.30) | collective-permute-done | bytes 524320 | tf_op jit(solution)/shard_map/ppermute | solution.py:25
  272.8 3.4 pack.13
  276.2 4.5 %all-to-all-start.2 = ((f32[4,16,64,128]{3,2,1,0:T(8,128)}), f32[4,16,64,128]{3,2,1,0:T(8,128)S(1)}, u32[]{:S(2)}, u32[]{:S(2)}) async-start(f32[4,16,64,128]{3,2,1,0:T(8,128)} %pack.13), calls=%async_computation.2 | async-start | bytes 4194304 | tf_op jit(solution)/shard_map/all_to_all | solution.py:34
  280.6 3.2 collective-permute-start.33
  285.4 8.4 %collective-permute-done.33.refs_1_ = f32[16,64,128]{2,1,0:T(8,128)S(1)} collective-permute-done((f32[16,64,128]{2,1,0:T(8,128)S(1)}, f32[16,64,128]{2,1,0:T(8,128)S(1)}, u32[]{:S(2)}, u32[]{:S(2)}) %collective-permute-start.33) | collective-permute-done | bytes 524320 | tf_op jit(solution)/shard_map/ppermute | solution.py:25
  293.8 3.7 collective-permute-start.38
  298.4 8.2 %collective-permute-done.38.refs_1_ = f32[16,64,128]{2,1,0:T(8,128)S(1)} collective-permute-done((f32[16,64,128]{2,1,0:T(8,128)S(1)}, f32[16,64,128]{2,1,0:T(8,128)S(1)}, u32[]{:S(2)}, u32[]{:S(2)}) %collective-permute-start.38) | collective-permute-done | bytes 524320 | tf_op jit(solution)/shard_map/ppermute | solution.py:25
  306.6 4.0 collective-permute-done.39.refs_2_
  310.6 3.9 pack.15
  315.9 5.2 %all-to-all-start.3 = ((f32[4,24,64,128]{3,2,1,0:T(8,128)}), f32[4,24,64,128]{3,2,1,0:T(8,128)S(1)}, u32[]{:S(2)}, u32[]{:S(2)}) async-start(f32[4,24,64,128]{3,2,1,0:T(8,128)} %pack.15), calls=%async_computation.3 | async-start | bytes 6291456 | tf_op jit(solution)/shard_map/all_to_all | solution.py:34
  321.1 2.8 pack.12
  323.9 2.0 collective-permute-start.27
  325.9 3.4 pack.14
  332.0 2.6 collective-permute-start.36
  335.5 29.9 %collective-permute-done.27.refs_3_ = f32[8,64,128]{2,1,0:T(8,128)S(1)} collective-permute-done((f32[8,64,128]{2,1,0:T(8,128)}, f32[8,64,128]{2,1,0:T(8,128)S(1)}, u32[]{:S(2)}, u32[]{:S(2)}) %collective-permute-start.27) | collective-permute-done | bytes 262176 | tf_op jit(solution)/shard_map/ppermute | solution.py:25
  366.3 22.9 %collective-permute-done.28.refs_4_ = f32[8,64,128]{2,1,0:T(8,128)S(1)} collective-permute-done((f32[8,64,128]{2,1,0:T(8,128)}, f32[8,64,128]{2,1,0:T(8,128)S(1)}, u32[]{:S(2)}, u32[]{:S(2)}) %collective-permute-start.28) | collective-permute-done | bytes 262176 | tf_op jit(solution)/shard_map/ppermute | solution.py:25
  392.5 15.0 %product.3 = f32[2,8,64,128]{3,2,1,0:T(8,128)} custom-call(s32[4]{0:T(128)} %pad_add_fusion.7.meta, s32[768]{0:T(1024)} %get-tuple-element.44.pos, f32[4,8,64,768]{3,2,1,0:T(8,128)} %pad_maximum_fusion.refs_0_, f32[4,8,64,768]{3,2,1,0:T(8,128)} %collective-permute-done.4.refs_1_, f32[8,64,128]{2,1,0:T(8,128)} %get-tuple-element.29.refs_2_, ...), custom_call_target="tpu_custom_call" | custom-call | tf_op jit(solution)/shard_map/product/pallas_call | solution.py:114
  (144 shorter events, 42.1 us)
Async XLA Ops:
  6.1 56.2 %copy-start.4 = (f32[8,64,768]{2,1,0:T(8,128)S(1)}, f32[8,64,768]{2,1,0:T(8,128)}, u32[]{:S(2)}) copy-start(f32[8,64,768]{2,1,0:T(8,128)} %turn.3) | copy-start | bytes 4718596
  6.1 36.3 %collective-permute-start.8 = (f32[8,64,768]{2,1,0:T(8,128)}, f32[8,64,768]{2,1,0:T(8,128)S(1)}, u32[]{:S(2)}, u32[]{:S(2)}) collective-permute-start(f32[8,64,768]{2,1,0:T(8,128)} %turn.3), channel_id=1, source_target_pairs={{0,1},{1,2},{2,3},{3,0},{4,5},{5,6},{6,7},{7,4},{8,9},{9,10},{10,1... | collective-permute-start | bytes 4718600 | tf_op jit(solution)/shard_map/ppermute | solution.py:29
  7.4 36.5 %collective-permute-start.9 = (f32[8,64,768]{2,1,0:T(8,128)}, f32[8,64,768]{2,1,0:T(8,128)S(1)}, u32[]{:S(2)}, u32[]{:S(2)}) collective-permute-start(f32[8,64,768]{2,1,0:T(8,128)} %turn.3), channel_id=1, source_target_pairs={{0,3},{1,0},{2,1},{3,2},{4,7},{5,4},{6,5},{7,6},{8,11},{9,8},{10,9... | collective-permute-start | bytes 4718600 | tf_op jit(solution)/shard_map/ppermute | solution.py:29
  42.5 18.5 %collective-permute-start.10 = (f32[4,64,768]{2,1,0:T(8,128)S(1)}, f32[4,64,768]{2,1,0:T(8,128)S(1)}, u32[]{:S(2)}, u32[]{:S(2)}) collective-permute-start(f32[4,64,768]{2,1,0:T(8,128)S(1)} %slice.78), channel_id=1, source_target_pairs={{0,1},{1,2},{2,3},{3,0},{4,5},{5,6},{6,7},{7,4},{8,9},{9,10},{10,1... | collective-permute-start | bytes 2359304 | tf_op jit(solution)/shard_map/ppermute | solution.py:29
  43.9 18.2 %collective-permute-start.11 = (f32[4,64,768]{2,1,0:T(8,128)S(1)}, f32[4,64,768]{2,1,0:T(8,128)S(1)}, u32[]{:S(2)}, u32[]{:S(2)}) collective-permute-start(f32[4,64,768]{2,1,0:T(8,128)S(1)} %slice.79), channel_id=1, source_target_pairs={{0,3},{1,0},{2,1},{3,2},{4,7},{5,4},{6,5},{7,6},{8,11},{9,8},{10,9... | collective-permute-start | bytes 2359304 | tf_op jit(solution)/shard_map/ppermute | solution.py:29
  62.3 35.8 %copy-start.23 = (s32[8,48]{1,0:T(8,128)S(1)}, s32[8,48]{1,0:T(8,128)}, u32[]{:S(2)}) copy-start(s32[8,48]{1,0:T(8,128)} %param.12) | copy-start | bytes 4612
  65.3 174.3 %collective-permute-start.12 = (f32[4,8,64,768]{3,2,1,0:T(8,128)}, f32[4,8,64,768]{3,2,1,0:T(8,128)}, u32[]{:S(2)}, u32[]{:S(2)}) collective-permute-start(f32[4,8,64,768]{3,2,1,0:T(8,128)} %pad_maximum_fusion.1.refs_0_), channel_id=1, source_target_pairs={{0,4},{4,0},{8,12},{12,8},{16,20},{20,16},{24,28},{28,24},{32,36},... | collective-permute-start | bytes 18874376 | tf_op jit(solution)/shard_map/ppermute | solution.py:25
  65.4 10.7 %collective-permute-start.13 = (f32[512,128]{1,0:T(8,128)S(1)}, f32[512,128]{1,0:T(8,128)S(1)}, u32[]{:S(2)}, u32[]{:S(2)}) collective-permute-start(f32[512,128]{1,0:T(8,128)S(1)} %get-tuple-element.40), channel_id=1, source_target_pairs={{0,4},{4,0},{8,12},{12,8},{16,20},{20,16},{24,28},{28,24},{32,36},... | collective-permute-start | bytes 786440 | tf_op jit(solution)/shard_map/ppermute | solution.py:25
  76.1 36.8 %copy-start.5 = (f32[1024,128]{1,0:T(8,128)}, f32[1024,128]{1,0:T(8,128)S(1)}, u32[]{:S(2)}) copy-start(f32[1024,128]{1,0:T(8,128)S(1)} %pad_maximum_fusion.2) | copy-start | bytes 1572868
  76.1 18.2 %collective-permute-start.17 = (f32[16,64,128]{2,1,0:T(8,128)S(1)}, f32[16,64,128]{2,1,0:T(8,128)S(1)}, u32[]{:S(2)}, u32[]{:S(2)}) collective-permute-start(f32[16,64,128]{2,1,0:T(8,128)S(1)} %bitcast.24), channel_id=1, source_target_pairs={{0,32},{4,36},{8,40},{12,44},{16,48},{20,52},{24,56},{28,60},{32,6... | collective-permute-start | bytes 1572872 | tf_op jit(solution)/shard_map/ppermute | solution.py:25
  78.1 16.7 %collective-permute-start.18 = (f32[16,64,128]{2,1,0:T(8,128)S(1)}, f32[16,64,128]{2,1,0:T(8,128)}, u32[]{:S(2)}, u32[]{:S(2)}) collective-permute-start(f32[16,64,128]{2,1,0:T(8,128)S(1)} %bitcast.25), channel_id=1, source_target_pairs={{0,224},{4,228},{8,232},{12,236},{16,240},{20,244},{24,248},{28,25... | collective-permute-start | bytes 1572872 | tf_op jit(solution)/shard_map/ppermute | solution.py:25
  94.3 14.6 %collective-permute-start.19 = (f32[16,64,128]{2,1,0:T(8,128)S(1)}, f32[16,64,128]{2,1,0:T(8,128)S(1)}, u32[]{:S(2)}, u32[]{:S(2)}) collective-permute-start(f32[16,64,128]{2,1,0:T(8,128)S(1)} %collective-permute-done.17.refs_0_), channel_id=1, source_target_pairs={{0,32},{4,36},{8,40},{12,44},{16,48},{20,52},{24,56},{28,60},{32,6... | collective-permute-start | bytes 1572872 | tf_op jit(solution)/shard_map/ppermute | solution.py:25
  94.8 31.4 %collective-permute-start.20 = (f32[16,64,128]{2,1,0:T(8,128)}, f32[16,64,128]{2,1,0:T(8,128)S(1)}, u32[]{:S(2)}, u32[]{:S(2)}) collective-permute-start(f32[16,64,128]{2,1,0:T(8,128)} %collective-permute-done.18.refs_1_), channel_id=1, source_target_pairs={{0,224},{4,228},{8,232},{12,236},{16,240},{20,244},{24,248},{28,25... | collective-permute-start | bytes 1572872 | tf_op jit(solution)/shard_map/ppermute | solution.py:25
  98.1 1.3 collective-permute-start
  99.4 4.1 %collective-permute-start.5 = (s32[4,128]{1,0:T(4,128)S(1)}, s32[4,128]{1,0:T(4,128)S(1)}, u32[]{:S(2)}, u32[]{:S(2)}) collective-permute-start(s32[4,128]{1,0:T(4,128)S(1)} %pad_add_fusion.6), channel_id=1, source_target_pairs={{0,24},{4,28},{8,0},{12,4},{16,8},{20,12},{24,16},{28,20},{32,56},... | collective-permute-start | bytes 6152 | tf_op jit(solution)/shard_map/ppermute | solution.py:25
  102.2 5.1 %collective-permute-start.6 = (s32[4,128]{1,0:T(4,128)S(1)}, s32[4,128]{1,0:T(4,128)S(1)}, u32[]{:S(2)}, u32[]{:S(2)}) collective-permute-start(s32[4,128]{1,0:T(4,128)S(1)} %pad_add_fusion.6), channel_id=1, source_target_pairs={{0,16},{4,20},{8,24},{12,28},{16,0},{20,4},{24,8},{28,12},{32,48},... | collective-permute-start | bytes 6152 | tf_op jit(solution)/shard_map/ppermute | solution.py:25
  103.5 5.0 %collective-permute-start.7 = (s32[4,128]{1,0:T(4,128)S(1)}, s32[4,128]{1,0:T(4,128)S(1)}, u32[]{:S(2)}, u32[]{:S(2)}) collective-permute-start(s32[4,128]{1,0:T(4,128)S(1)} %pad_add_fusion.6), channel_id=1, source_target_pairs={{0,8},{4,12},{8,16},{12,20},{16,24},{20,28},{24,0},{28,4},{32,40},... | collective-permute-start | bytes 6152 | tf_op jit(solution)/shard_map/ppermute | solution.py:25
  108.9 19.6 %collective-permute-start.24 = (f32[16,64,128]{2,1,0:T(8,128)S(1)}, f32[16,64,128]{2,1,0:T(8,128)}, u32[]{:S(2)}, u32[]{:S(2)}) collective-permute-start(f32[16,64,128]{2,1,0:T(8,128)S(1)} %collective-permute-done.19.refs_0_), channel_id=1, source_target_pairs={{0,32},{4,36},{8,40},{12,44},{16,48},{20,52},{24,56},{28,60},{32,6... | collective-permute-start | bytes 1572872 | tf_op jit(solution)/shard_map/ppermute | solution.py:25
  112.9 44.2 %all-to-all-start = ((f32[4,16,64,128]{3,2,1,0:T(8,128)}), f32[4,16,64,128]{3,2,1,0:T(8,128)S(1)}, u32[]{:S(2)}, u32[]{:S(2)}) async-start(f32[4,16,64,128]{3,2,1,0:T(8,128)} %pack.9), calls=%async_computation | async-start | bytes 4194304 | tf_op jit(solution)/shard_map/all_to_all | solution.py:34
  123.3 39.3 %collective-permute-start.1 = (f32[8,64,768]{2,1,0:T(8,128)}, f32[8,64,768]{2,1,0:T(8,128)}, u32[]{:S(2)}, u32[]{:S(2)}) collective-permute-start(f32[8,64,768]{2,1,0:T(8,128)} %turn.2), channel_id=1, source_target_pairs={{0,1},{1,2},{2,3},{3,0},{4,5},{5,6},{6,7},{7,4},{8,9},{9,10},{10,1... | collective-permute-start | bytes 4718600 | tf_op jit(solution)/shard_map/ppermute | solution.py:29
  126.2 37.6 %collective-permute-start.2 = (f32[8,64,768]{2,1,0:T(8,128)}, f32[8,64,768]{2,1,0:T(8,128)}, u32[]{:S(2)}, u32[]{:S(2)}) collective-permute-start(f32[8,64,768]{2,1,0:T(8,128)} %turn.2), channel_id=1, source_target_pairs={{0,3},{1,0},{2,1},{3,2},{4,7},{5,4},{6,5},{7,6},{8,11},{9,8},{10,9... | collective-permute-start | bytes 4718600 | tf_op jit(solution)/shard_map/ppermute | solution.py:29
  126.2 66.3 %collective-permute-start.3 = (f32[8,64,768]{2,1,0:T(8,128)}, f32[8,64,768]{2,1,0:T(8,128)}, u32[]{:S(2)}, u32[]{:S(2)}) collective-permute-start(f32[8,64,768]{2,1,0:T(8,128)} %turn.2), channel_id=1, source_target_pairs={{0,2},{1,3},{2,0},{3,1},{4,6},{5,7},{6,4},{7,5},{8,10},{9,11},{10,... | collective-permute-start | bytes 4718600 | tf_op jit(solution)/shard_map/ppermute | solution.py:29
  128.4 12.0 %collective-permute-start.25 = (f32[16,64,128]{2,1,0:T(8,128)S(1)}, f32[16,64,128]{2,1,0:T(8,128)S(1)}, u32[]{:S(2)}, u32[]{:S(2)}) collective-permute-start(f32[16,64,128]{2,1,0:T(8,128)S(1)} %collective-permute-done.20.refs_1_), channel_id=1, source_target_pairs={{0,224},{4,228},{8,232},{12,236},{16,240},{20,244},{24,248},{28,25... | collective-permute-start | bytes 1572872 | tf_op jit(solution)/shard_map/ppermute | solution.py:25
  140.4 12.7 %collective-permute-start.26 = (f32[16,64,128]{2,1,0:T(8,128)}, f32[16,64,128]{2,1,0:T(8,128)}, u32[]{:S(2)}, u32[]{:S(2)}) collective-permute-start(f32[16,64,128]{2,1,0:T(8,128)} %collective-permute-done.24.refs_0_), channel_id=1, source_target_pairs={{0,32},{4,36},{8,40},{12,44},{16,48},{20,52},{24,56},{28,60},{32,6... | collective-permute-start | bytes 1572872 | tf_op jit(solution)/shard_map/ppermute | solution.py:25
  158.4 81.2 %all-to-all-start.1 = ((f32[4,24,64,128]{3,2,1,0:T(8,128)}), f32[4,24,64,128]{3,2,1,0:T(8,128)S(1)}, u32[]{:S(2)}, u32[]{:S(2)}) async-start(f32[4,24,64,128]{3,2,1,0:T(8,128)} %pack.11), calls=%async_computation.1 | async-start | bytes 6291456 | tf_op jit(solution)/shard_map/all_to_all | solution.py:34
  197.2 137.4 %collective-permute-start.4 = (f32[4,8,64,768]{3,2,1,0:T(8,128)}, f32[4,8,64,768]{3,2,1,0:T(8,128)}, u32[]{:S(2)}, u32[]{:S(2)}) collective-permute-start(f32[4,8,64,768]{3,2,1,0:T(8,128)} %pad_maximum_fusion.refs_0_), channel_id=1, source_target_pairs={{0,4},{4,0},{8,12},{12,8},{16,20},{20,16},{24,28},{28,24},{32,36},... | collective-permute-start | bytes 18874376 | tf_op jit(solution)/shard_map/ppermute | solution.py:25
  200.1 10.1 %collective-permute-start.14 = (f32[8,64,128]{2,1,0:T(8,128)}, f32[8,64,128]{2,1,0:T(8,128)S(1)}, u32[]{:S(2)}, u32[]{:S(2)}) collective-permute-start(f32[8,64,128]{2,1,0:T(8,128)} %get-tuple-element.22), channel_id=1, source_target_pairs={{0,8},{4,12},{8,16},{12,20},{16,24},{20,28},{24,0},{28,4},{32,40},... | collective-permute-start | bytes 786440 | tf_op jit(solution)/shard_map/ppermute | solution.py:25
  201.8 15.8 %collective-permute-start.15 = (f32[8,64,128]{2,1,0:T(8,128)}, f32[8,64,128]{2,1,0:T(8,128)}, u32[]{:S(2)}, u32[]{:S(2)}) collective-permute-start(f32[8,64,128]{2,1,0:T(8,128)} %get-tuple-element.23), channel_id=1, source_target_pairs={{0,16},{4,20},{8,24},{12,28},{16,0},{20,4},{24,8},{28,12},{32,48},... | collective-permute-start | bytes 786440 | tf_op jit(solution)/shard_map/ppermute | solution.py:25
  204.5 14.0 %collective-permute-start.16 = (f32[8,64,128]{2,1,0:T(8,128)}, f32[8,64,128]{2,1,0:T(8,128)}, u32[]{:S(2)}, u32[]{:S(2)}) collective-permute-start(f32[8,64,128]{2,1,0:T(8,128)} %get-tuple-element.24), channel_id=1, source_target_pairs={{0,24},{4,28},{8,0},{12,4},{16,8},{20,12},{24,16},{28,20},{32,56},... | collective-permute-start | bytes 786440 | tf_op jit(solution)/shard_map/ppermute | solution.py:25
  210.2 18.6 %collective-permute-start.21 = (f32[16,64,128]{2,1,0:T(8,128)}, f32[16,64,128]{2,1,0:T(8,128)}, u32[]{:S(2)}, u32[]{:S(2)}) collective-permute-start(f32[16,64,128]{2,1,0:T(8,128)} %get-tuple-element.26), channel_id=1, source_target_pairs={{0,8},{4,12},{8,16},{12,20},{16,24},{20,28},{24,0},{28,4},{32,40},... | collective-permute-start | bytes 1572872 | tf_op jit(solution)/shard_map/ppermute | solution.py:25
  217.6 22.0 %collective-permute-start.22 = (f32[16,64,128]{2,1,0:T(8,128)}, f32[16,64,128]{2,1,0:T(8,128)}, u32[]{:S(2)}, u32[]{:S(2)}) collective-permute-start(f32[16,64,128]{2,1,0:T(8,128)} %get-tuple-element.27), channel_id=1, source_target_pairs={{0,16},{4,20},{8,24},{12,28},{16,0},{20,4},{24,8},{28,12},{32,48},... | collective-permute-start | bytes 1572872 | tf_op jit(solution)/shard_map/ppermute | solution.py:25
  218.5 21.1 %collective-permute-start.23 = (f32[16,64,128]{2,1,0:T(8,128)}, f32[16,64,128]{2,1,0:T(8,128)}, u32[]{:S(2)}, u32[]{:S(2)}) collective-permute-start(f32[16,64,128]{2,1,0:T(8,128)} %get-tuple-element.28), channel_id=1, source_target_pairs={{0,24},{4,28},{8,0},{12,4},{16,8},{20,12},{24,16},{28,20},{32,56},... | collective-permute-start | bytes 1572872 | tf_op jit(solution)/shard_map/ppermute | solution.py:25
  256.3 15.1 %collective-permute-start.30 = (f32[16,64,128]{2,1,0:T(8,128)}, f32[16,64,128]{2,1,0:T(8,128)}, u32[]{:S(2)}, u32[]{:S(2)}) collective-permute-start(f32[16,64,128]{2,1,0:T(8,128)} %bitcast.21), channel_id=1, source_target_pairs={{0,32},{4,36},{8,40},{12,44},{16,48},{20,52},{24,56},{28,60},{32,6... | collective-permute-start | bytes 1572872 | tf_op jit(solution)/shard_map/ppermute | solution.py:25
  256.4 15.6 %collective-permute-start.31 = (f32[16,64,128]{2,1,0:T(8,128)}, f32[16,64,128]{2,1,0:T(8,128)S(1)}, u32[]{:S(2)}, u32[]{:S(2)}) collective-permute-start(f32[16,64,128]{2,1,0:T(8,128)} %bitcast.22), channel_id=1, source_target_pairs={{0,224},{4,228},{8,232},{12,236},{16,240},{20,244},{24,248},{28,25... | collective-permute-start | bytes 1572872 | tf_op jit(solution)/shard_map/ppermute | solution.py:25
  271.4 14.0 %collective-permute-start.32 = (f32[16,64,128]{2,1,0:T(8,128)}, f32[16,64,128]{2,1,0:T(8,128)S(1)}, u32[]{:S(2)}, u32[]{:S(2)}) collective-permute-start(f32[16,64,128]{2,1,0:T(8,128)} %collective-permute-done.30.refs_0_), channel_id=1, source_target_pairs={{0,32},{4,36},{8,40},{12,44},{16,48},{20,52},{24,56},{28,60},{32,6... | collective-permute-start | bytes 1572872 | tf_op jit(solution)/shard_map/ppermute | solution.py:25
  276.2 38.4 %all-to-all-start.2 = ((f32[4,16,64,128]{3,2,1,0:T(8,128)}), f32[4,16,64,128]{3,2,1,0:T(8,128)S(1)}, u32[]{:S(2)}, u32[]{:S(2)}) async-start(f32[4,16,64,128]{3,2,1,0:T(8,128)} %pack.13), calls=%async_computation.2 | async-start | bytes 4194304 | tf_op jit(solution)/shard_map/all_to_all | solution.py:34
  280.6 13.2 %collective-permute-start.33 = (f32[16,64,128]{2,1,0:T(8,128)S(1)}, f32[16,64,128]{2,1,0:T(8,128)S(1)}, u32[]{:S(2)}, u32[]{:S(2)}) collective-permute-start(f32[16,64,128]{2,1,0:T(8,128)S(1)} %copy-done.15), channel_id=1, source_target_pairs={{0,224},{4,228},{8,232},{12,236},{16,240},{20,244},{24,248},{28,25... | collective-permute-start | bytes 1572872 | tf_op jit(solution)/shard_map/ppermute | solution.py:25
  285.4 13.0 %collective-permute-start.37 = (f32[16,64,128]{2,1,0:T(8,128)S(1)}, f32[16,64,128]{2,1,0:T(8,128)S(1)}, u32[]{:S(2)}, u32[]{:S(2)}) collective-permute-start(f32[16,64,128]{2,1,0:T(8,128)S(1)} %collective-permute-done.32.refs_0_), channel_id=1, source_target_pairs={{0,32},{4,36},{8,40},{12,44},{16,48},{20,52},{24,56},{28,60},{32,6... | collective-permute-start | bytes 1572872 | tf_op jit(solution)/shard_map/ppermute | solution.py:25
  293.8 12.8 %collective-permute-start.38 = (f32[16,64,128]{2,1,0:T(8,128)S(1)}, f32[16,64,128]{2,1,0:T(8,128)S(1)}, u32[]{:S(2)}, u32[]{:S(2)}) collective-permute-start(f32[16,64,128]{2,1,0:T(8,128)S(1)} %collective-permute-done.33.refs_1_), channel_id=1, source_target_pairs={{0,224},{4,228},{8,232},{12,236},{16,240},{20,244},{24,248},{28,25... | collective-permute-start | bytes 1572872 | tf_op jit(solution)/shard_map/ppermute | solution.py:25
  298.4 12.2 %collective-permute-start.39 = (f32[16,64,128]{2,1,0:T(8,128)S(1)}, f32[16,64,128]{2,1,0:T(8,128)}, u32[]{:S(2)}, u32[]{:S(2)}) collective-permute-start(f32[16,64,128]{2,1,0:T(8,128)S(1)} %collective-permute-done.37.refs_0_), channel_id=1, source_target_pairs={{0,32},{4,36},{8,40},{12,44},{16,48},{20,52},{24,56},{28,60},{32,6... | collective-permute-start | bytes 1572872 | tf_op jit(solution)/shard_map/ppermute | solution.py:25
  315.9 75.0 %all-to-all-start.3 = ((f32[4,24,64,128]{3,2,1,0:T(8,128)}), f32[4,24,64,128]{3,2,1,0:T(8,128)S(1)}, u32[]{:S(2)}, u32[]{:S(2)}) async-start(f32[4,24,64,128]{3,2,1,0:T(8,128)} %pack.15), calls=%async_computation.3 | async-start | bytes 6291456 | tf_op jit(solution)/shard_map/all_to_all | solution.py:34
  323.9 41.5 %collective-permute-start.27 = (f32[8,64,128]{2,1,0:T(8,128)}, f32[8,64,128]{2,1,0:T(8,128)S(1)}, u32[]{:S(2)}, u32[]{:S(2)}) collective-permute-start(f32[8,64,128]{2,1,0:T(8,128)} %get-tuple-element.30), channel_id=1, source_target_pairs={{0,8},{4,12},{8,16},{12,20},{16,24},{20,28},{24,0},{28,4},{32,40},... | collective-permute-start | bytes 786440 | tf_op jit(solution)/shard_map/ppermute | solution.py:25
  329.3 59.8 %collective-permute-start.34 = (f32[16,64,128]{2,1,0:T(8,128)}, f32[16,64,128]{2,1,0:T(8,128)S(1)}, u32[]{:S(2)}, u32[]{:S(2)}) collective-permute-start(f32[16,64,128]{2,1,0:T(8,128)} %get-tuple-element.34), channel_id=1, source_target_pairs={{0,8},{4,12},{8,16},{12,20},{16,24},{20,28},{24,0},{28,4},{32,40},... | collective-permute-start | bytes 1572872 | tf_op jit(solution)/shard_map/ppermute | solution.py:25
  330.8 58.4 %collective-permute-start.35 = (f32[16,64,128]{2,1,0:T(8,128)}, f32[16,64,128]{2,1,0:T(8,128)S(1)}, u32[]{:S(2)}, u32[]{:S(2)}) collective-permute-start(f32[16,64,128]{2,1,0:T(8,128)} %get-tuple-element.35), channel_id=1, source_target_pairs={{0,16},{4,20},{8,24},{12,28},{16,0},{20,4},{24,8},{28,12},{32,48},... | collective-permute-start | bytes 1572872 | tf_op jit(solution)/shard_map/ppermute | solution.py:25
  332.0 58.9 %collective-permute-start.36 = (f32[16,64,128]{2,1,0:T(8,128)}, f32[16,64,128]{2,1,0:T(8,128)}, u32[]{:S(2)}, u32[]{:S(2)}) collective-permute-start(f32[16,64,128]{2,1,0:T(8,128)} %get-tuple-element.36), channel_id=1, source_target_pairs={{0,24},{4,28},{8,0},{12,4},{16,8},{20,12},{24,16},{28,20},{32,56},... | collective-permute-start | bytes 1572872 | tf_op jit(solution)/shard_map/ppermute | solution.py:25
  334.6 54.5 %collective-permute-start.28 = (f32[8,64,128]{2,1,0:T(8,128)}, f32[8,64,128]{2,1,0:T(8,128)S(1)}, u32[]{:S(2)}, u32[]{:S(2)}) collective-permute-start(f32[8,64,128]{2,1,0:T(8,128)} %get-tuple-element.31), channel_id=1, source_target_pairs={{0,16},{4,20},{8,24},{12,28},{16,0},{20,4},{24,8},{28,12},{32,48},... | collective-permute-start | bytes 786440 | tf_op jit(solution)/shard_map/ppermute | solution.py:25
  365.4 23.8 %collective-permute-start.29 = (f32[8,64,128]{2,1,0:T(8,128)}, f32[8,64,128]{2,1,0:T(8,128)S(1)}, u32[]{:S(2)}, u32[]{:S(2)}) collective-permute-start(f32[8,64,128]{2,1,0:T(8,128)} %get-tuple-element.32), channel_id=1, source_target_pairs={{0,24},{4,28},{8,0},{12,4},{16,8},{20,12},{24,16},{28,20},{32,56},... | collective-permute-start | bytes 786440 | tf_op jit(solution)/shard_map/ppermute | solution.py:25
  408.6 1.6 collective-permute-start.40
  (24 other events, 281.2 us)

commit v2 on v1

--- a/solution.py
+++ b/solution.py
@@ -12,6 +12,7 @@
 GROUPS = ((0,), (7, 1), (6, 2), (5, 3, 4))
 
 STARTS = (0, 1, 3, 5)
+EARLY, LATE = 40, 24
 WHOLE = (False, True, False, True)
 
 
@@ -65,33 +66,79 @@
     )(meta, fetch, *pieces)
 
 
-def product_kernel(meta, pos, *refs):
-    arrived = iter(refs[2:-4])
-    out, slabs, split, sems = refs[-4:]
-    x, y = meta[1], meta[3]
+def split_in_two(value, ref, *at):
+    high = value.astype(jnp.bfloat16)
+    ref[*at, :, :HALF] = high
+    ref[*at, :, HALF:] = (value - high.astype(jnp.float32)).astype(jnp.bfloat16)
+
+
+def early_kernel(meta, *refs):
+    arrived = iter(refs[:-3])
+    out, slabs, sems = refs[-3:]
+    x = meta[1]
     step = pl.program_id(0)
 
     @pl.when(step == 0)
     def _():
-        for g, offsets in enumerate(GROUPS):
+        for g, offsets in enumerate(GROUPS[:-1]):
             block = next(arrived) if WHOLE[g] else None
             for s in range(NX):
                 xp = (x - s) & 3
                 part = block.at[xp] if WHOLE[g] else next(arrived)
                 n = len(offsets) * 8
-                pltpu.make_async_copy(part, slabs.at[pl.ds(xp * 64 + STARTS[g] * 8, n)], sems.at[xp]).start()
-        for xp in range(NX):
-            part = slabs.at[pl.ds(xp * 64, 64)]
+                pltpu.make_async_copy(part, slabs.at[pl.ds(xp * EARLY + STARTS[g] * 8, n)], sems.at[xp]).start()
+
+    part = slabs.at[pl.ds(step * EARLY, EARLY)]
+    pltpu.make_async_copy(part, part, sems.at[step]).wait()
+
+    def convert(i, carry):
+        split_in_two(slabs[step * EARLY + i], out, 0, i)
+        return carry
+
+    lax.fori_loop(0, EARLY, convert, 0, unroll=4)
+
+
+def early_product(meta, arrived):
+    return pl.pallas_call(
+        early_kernel,
+        out_shape=jax.ShapeDtypeStruct((NX, EARLY, B, 2 * HALF), jnp.bfloat16),
+        grid_spec=pltpu.PrefetchScalarGridSpec(
+            num_scalar_prefetch=1,
+            grid=(NX,),
+            in_specs=[pl.BlockSpec(memory_space=pl.ANY)] * len(arrived),
+            out_specs=pl.BlockSpec((1, EARLY, B, 2 * HALF), lambda i, *_: (i, 0, 0, 0)),
+            scratch_shapes=[
+                pltpu.VMEM((NX * EARLY, B, HALF), jnp.float32),
+                pltpu.SemaphoreType.DMA((NX,)),
+            ],
+        ),
+        name="early",
+    )(meta, *arrived)
+
+
+def product_kernel(meta, pos, *refs):
+    early, arrived, out, slabs, split, early_sems, sems = refs[2:]
+    y = meta[3]
+    step = pl.program_id(0)
+
+    @pl.when(step == 0)
+    def _():
+        for xp in range(NX):
+            pltpu.make_async_copy(arrived.at[xp], slabs.at[pl.ds(xp * LATE, LATE)], sems.at[xp]).start()
+        for xp in range(NX):
+            pltpu.make_async_copy(early.at[xp], split.at[pl.ds(xp * 64, EARLY)], early_sems.at[xp]).start()
+        for xp in range(NX):
+            part = slabs.at[pl.ds(xp * LATE, LATE)]
             pltpu.make_async_copy(part, part, sems.at[xp]).wait()
 
-            def convert(i, carry):
-                value = slabs[i]
-                high = value.astype(jnp.bfloat16)
-                split[i, :, :HALF] = high
-                split[i, :, HALF:] = (value - high.astype(jnp.float32)).astype(jnp.bfloat16)
+            def convert(i, carry, xp=xp):
+                split_in_two(slabs[xp * LATE + i], split, xp * 64 + EARLY + i)
                 return carry
 
-            lax.fori_loop(xp * 64, xp * 64 + 64, convert, 0, unroll=4)
+            lax.fori_loop(0, LATE, convert, 0, unroll=4)
+        for xp in range(NX):
+            part = split.at[pl.ds(xp * 64, EARLY)]
+            pltpu.make_async_copy(part, part, early_sems.at[xp]).wait()
 
     for l, blocks in enumerate(refs[:2]):
         total = jnp.zeros((2 * B, 2 * HALF), jnp.float32)
@@ -108,7 +155,7 @@
         out[l, 0] = upper[:, :HALF] + (upper[:, HALF:] + (lower[:, :HALF] + lower[:, HALF:]))
 
 
-def product(meta, pos, own_blocks, partner_blocks, arrived):
+def product(meta, pos, own_blocks, partner_blocks, early, arrived):
     block = pl.BlockSpec((4, 1, B, 768), lambda i, *_: (0, i, 0, 0))
     anywhere = pl.BlockSpec(memory_space=pl.ANY)
     return pl.pallas_call(
@@ -117,16 +164,17 @@
         grid_spec=pltpu.PrefetchScalarGridSpec(
             num_scalar_prefetch=2,
             grid=(8,),
-            in_specs=[block] * 2 + [anywhere] * len(arrived),
+            in_specs=[block] * 2 + [anywhere] * 2,
             out_specs=pl.BlockSpec((2, 1, B, HALF), lambda i, *_: (0, i, 0, 0)),
             scratch_shapes=[
-                pltpu.VMEM((256, B, HALF), jnp.float32),
+                pltpu.VMEM((NX * LATE, B, HALF), jnp.float32),
                 pltpu.VMEM((256, B, 2 * HALF), jnp.bfloat16),
+                pltpu.SemaphoreType.DMA((NX,)),
                 pltpu.SemaphoreType.DMA((NX,)),
             ],
         ),
         name="product",
-    )(meta, pos, own_blocks, partner_blocks, *arrived)
+    )(meta, pos, own_blocks, partner_blocks, early, arrived)
 
 
 def fetch_rows(own, meta, fetch_x):
@@ -199,7 +247,9 @@
     )
     other = rows_shift(numbers, dc=1)
     lists = jnp.concatenate([numbers[:2], other[:2]], axis=0)
-    along = [lists] + [rows_shift(lists, dx=-s) for s in range(1, 4)]
+    along = [lists]
+    for s in range(1, NX):
+        along.append(rows_shift(lists, dx=-s))
 
     left, right = p_panel[:, :HALF], p_panel[:, HALF:]
     keep, give = jnp.where(c == 0, left, right), jnp.where(c == 0, right, left)
@@ -213,7 +263,8 @@
         low = 2 + 8 * n
         pos = positions(jnp.concatenate([numbers[low : low + 8, :48], other[low : low + 8, :48]], axis=0), z, c)
         arrived = fetch_rows(own, meta, fetch_x)
-        own = product(meta, pos, *with_partner(blocks[n]), arrived).reshape(16, B, HALF)
+        early = early_product(meta, arrived[:-1])
+        own = product(meta, pos, *with_partner(blocks[n]), early, arrived[-1]).reshape(16, B, HALF)
 
     result = own.reshape(2, 512, HALF)
     back = rows_shift(result[1], dc=1)

time: 417 us -> 426 us (1.022)
  Pallas kernels: 69.3 us -> 78.8 us
    pallas_call x0 -> x2, Pallas kernels: none -> 11.7 us  [early_product(): pl.pallas_call(early_kernel, out_shape=jax.ShapeDtypeStruct((NX, EARLY, B...]
    unnamed x56 -> x48, local copies, waits for them, and re-layouts: 8.7 us -> 7.02 us
  transfers between devices with their start and end apart: 45 -> 45, of which waited for: 27 -> 28; matrix products, arithmetic and copies ran while one was open for 2% -> 2% of each run, Pallas kernels for 12% -> 14%
where the time goes in v2:
time: 426 us; the launch traced here: 419 us
  waiting for transfers between devices  247 us (58%)
  Pallas kernels  78.8 us (18%)
  starting transfers between devices  73.3 us (17%)
  other arithmetic  11.3 us (3%)
  local copies, waits for them, and re-layouts  8.9 us (2%)
    ppermute x34, waiting for transfers between devices, rows_shift(): return lax.ppermute(array, 'rows', pairs)  165 us
    ppermute x7, waiting for transfers between devices, cols_shift(): return lax.ppermute(array, 'cols', [(y, (y + dy) % NY) for y in range(NY)])  81.6 us
    ppermute x34, starting transfers between devices, rows_shift(): return lax.ppermute(array, 'rows', pairs)  45.9 us
    pallas_call x2, Pallas kernels, product(): pl.pallas_call(product_kernel, out_shape=jax.ShapeDtypeStruct((2, 8, B, H...  27.8 us
    pallas_call x8, Pallas kernels, pack(): pl.pallas_call(functools.partial(pack_kernel, offsets, whole), out_shape=...  27.1 us
    all_to_all x4, starting transfers between devices, x_exchange(): lax.all_to_all(array, 'rows', 0, 0, axis_index_groups=groups, tiled=True)  18.2 us
    pallas_call x2, Pallas kernels, gather_blocks(): pl.pallas_call(turn_kernel, out_shape=jax.ShapeDtypeStruct((8, B, 768), j...  12.2 us
    pallas_call x2, Pallas kernels, early_product(): pl.pallas_call(early_kernel, out_shape=jax.ShapeDtypeStruct((NX, EARLY, B...  11.7 us
  transfers between devices with their start and end apart: 45, of which 28 were waited for; matrix products, arithmetic and copies ran while one was open for 2% of the time, Pallas kernels for 14%

profile of v2, /device:TPU:16, one launch (start us, length us, event | category | flops | bytes accessed | tf_op | source)
XLA Modules:
  0.0 419.2 jit_solution(12894141269545980750)
XLA Ops:
  0.0 6.1 %turn.3 = f32[8,64,768]{2,1,0:T(8,128)} custom-call(f32[8,12,64,64]{3,2,1,0:T(8,128)} %blocks.3), custom_call_target="tpu_custom_call" | custom-call | tf_op jit(solution)/shard_map/turn/pallas_call | solution.py:206
  8.1 34.3 %collective-permute-done.8 = f32[8,64,768]{2,1,0:T(8,128)S(1)} collective-permute-done((f32[8,64,768]{2,1,0:T(8,128)}, f32[8,64,768]{2,1,0:T(8,128)S(1)}, u32[]{:S(2)}, u32[]{:S(2)}) %collective-permute-start.8) | collective-permute-done | bytes 1572896 | tf_op jit(solution)/shard_map/ppermute | solution.py:30
  44.8 16.3 %collective-permute-done.10 = f32[4,64,768]{2,1,0:T(8,128)S(1)} collective-permute-done((f32[4,64,768]{2,1,0:T(8,128)S(1)}, f32[4,64,768]{2,1,0:T(8,128)S(1)}, u32[]{:S(2)}, u32[]{:S(2)}) %collective-permute-start.10) | collective-permute-done | bytes 786464 | tf_op jit(solution)/shard_map/ppermute | solution.py:30
  62.4 3.0 pad_maximum_fusion.1.refs_0_
  66.0 10.1 %collective-permute-done.13 = f32[512,128]{1,0:T(8,128)S(1)} collective-permute-done((f32[512,128]{1,0:T(8,128)S(1)}, f32[512,128]{1,0:T(8,128)S(1)}, u32[]{:S(2)}, u32[]{:S(2)}) %collective-permute-start.13) | collective-permute-done | bytes 262176 | tf_op jit(solution)/shard_map/ppermute | solution.py:26
  78.1 4.0 collective-permute-start.18
  82.2 12.1 %collective-permute-done.17.refs_0_ = f32[16,64,128]{2,1,0:T(8,128)S(1)} collective-permute-done((f32[16,64,128]{2,1,0:T(8,128)S(1)}, f32[16,64,128]{2,1,0:T(8,128)S(1)}, u32[]{:S(2)}, u32[]{:S(2)}) %collective-permute-start.17) | collective-permute-done | bytes 524320 | tf_op jit(solution)/shard_map/ppermute | solution.py:26
  96.1 2.8 collective-permute-start.5
  101.3 3.2 collective-permute-start.20
  105.3 3.6 collective-permute-done.19.refs_0_
  109.6 3.4 pack.9
  113.0 4.3 %all-to-all-start = ((f32[4,16,64,128]{3,2,1,0:T(8,128)}), f32[4,16,64,128]{3,2,1,0:T(8,128)S(1)}, u32[]{:S(2)}, u32[]{:S(2)}) async-start(f32[4,16,64,128]{3,2,1,0:T(8,128)} %pack.9), calls=%async_computation | async-start | bytes 4194304 | tf_op jit(solution)/shard_map/all_to_all | solution.py:35
  117.2 6.1 %turn.2 = f32[8,64,768]{2,1,0:T(8,128)} custom-call(f32[8,12,64,64]{3,2,1,0:T(8,128)} %blocks.2), custom_call_target="tpu_custom_call" | custom-call | tf_op jit(solution)/shard_map/turn/pallas_call | solution.py:206
  123.3 2.9 collective-permute-start.1
  128.5 3.2 collective-permute-start.25
  131.7 8.8 %collective-permute-done.25.refs_1_ = f32[16,64,128]{2,1,0:T(8,128)S(1)} collective-permute-done((f32[16,64,128]{2,1,0:T(8,128)S(1)}, f32[16,64,128]{2,1,0:T(8,128)S(1)}, u32[]{:S(2)}, u32[]{:S(2)}) %collective-permute-start.25) | collective-permute-done | bytes 524320 | tf_op jit(solution)/shard_map/ppermute | solution.py:26
  140.5 12.7 %collective-permute-done.26.refs_2_ = f32[16,64,128]{2,1,0:T(8,128)} collective-permute-done((f32[16,64,128]{2,1,0:T(8,128)}, f32[16,64,128]{2,1,0:T(8,128)}, u32[]{:S(2)}, u32[]{:S(2)}) %collective-permute-start.26) | collective-permute-done | bytes 524320 | tf_op jit(solution)/shard_map/ppermute | solution.py:26
  153.1 3.9 pack.11
  158.4 4.2 %all-to-all-start.1 = ((f32[4,24,64,128]{3,2,1,0:T(8,128)}), f32[4,24,64,128]{3,2,1,0:T(8,128)S(1)}, u32[]{:S(2)}, u32[]{:S(2)}) async-start(f32[4,24,64,128]{3,2,1,0:T(8,128)} %pack.11), calls=%async_computation.1 | async-start | bytes 6291456 | tf_op jit(solution)/shard_map/all_to_all | solution.py:35
  163.8 28.7 %collective-permute-done.3 = f32[8,64,768]{2,1,0:T(8,128)} collective-permute-done((f32[8,64,768]{2,1,0:T(8,128)}, f32[8,64,768]{2,1,0:T(8,128)}, u32[]{:S(2)}, u32[]{:S(2)}) %collective-permute-start.3) | collective-permute-done | bytes 1572896 | tf_op jit(solution)/shard_map/ppermute | solution.py:30
  192.5 4.8 %pad_maximum_fusion.refs_0_ = f32[4,8,64,768]{3,2,1,0:T(8,128)} fusion(f32[1,8,64,768]{3,2,1,0:T(8,128)} %bitcast.7, f32[1,8,64,768]{3,2,1,0:T(8,128)} %bitcast.6, f32[1,8,64,768]{3,2,1,0:T(8,128)} %bitcast.5, f32[1,8,64,768]{3,2,1,0:T(8,128)} %bitcast.17), kind=kLoop, calls=%fused_computation | loop fusion | flops 4718592 | bytes 12582912 | tf_op jit(solution)/shard_map/stack | solution.py:226
  197.3 2.8 pack.8
  201.8 2.7 collective-permute-start.15
  206.1 3.4 pack.10
  211.2 6.4 %collective-permute-done.15.refs_2_ = f32[8,64,128]{2,1,0:T(8,128)} collective-permute-done((f32[8,64,128]{2,1,0:T(8,128)}, f32[8,64,128]{2,1,0:T(8,128)}, u32[]{:S(2)}, u32[]{:S(2)}) %collective-permute-start.15) | collective-permute-done | bytes 262176 | tf_op jit(solution)/shard_map/ppermute | solution.py:26
  220.7 8.1 %collective-permute-done.21.refs_6_ = f32[16,64,128]{2,1,0:T(8,128)} collective-permute-done((f32[16,64,128]{2,1,0:T(8,128)}, f32[16,64,128]{2,1,0:T(8,128)}, u32[]{:S(2)}, u32[]{:S(2)}) %collective-permute-start.21) | collective-permute-done | bytes 524320 | tf_op jit(solution)/shard_map/ppermute | solution.py:26
  228.8 10.9 %collective-permute-done.22.refs_7_ = f32[16,64,128]{2,1,0:T(8,128)} collective-permute-done((f32[16,64,128]{2,1,0:T(8,128)}, f32[16,64,128]{2,1,0:T(8,128)}, u32[]{:S(2)}, u32[]{:S(2)}) %collective-permute-start.22) | collective-permute-done | bytes 524320 | tf_op jit(solution)/shard_map/ppermute | solution.py:26
  239.6 5.8 %early.2.refs_2_ = bf16[4,40,64,256]{3,2,1,0:T(8,128)(2,1)} custom-call(s32[4]{0:T(128)} %pad_add_fusion.7.meta, f32[8,64,128]{2,1,0:T(8,128)} %get-tuple-element.21.refs_0_, f32[8,64,128]{2,1,0:T(8,128)} %copy-done.17, f32[8,64,128]{2,1,0:T(8,128)} %collective-permute-done.15.refs_2_, f32[8,64,128]{2,1,0:T(8,128)} %collective-permute-done.16.refs_3_, ...), custom_call_target="tpu_custom_call" | custom-call | tf_op jit(solution)/shard_map/early/pallas_call | solution.py:102
  247.1 13.9 %product.2 = f32[2,8,64,128]{3,2,1,0:T(8,128)} custom-call(s32[4]{0:T(128)} %pad_add_fusion.7.meta, s32[768]{0:T(1024)} %get-tuple-element.43.pos, f32[4,8,64,768]{3,2,1,0:T(8,128)} %pad_maximum_fusion.1.refs_0_, f32[4,8,64,768]{3,2,1,0:T(8,128)} %collective-permute-done.12.refs_1_, bf16[4,40,64,256]{3,2,1,0:T(8,128)(2,1)} %early.2.refs_2_, ...), custom_call_target="tpu_custom_call" | custom-call | tf_op jit(solution)/shard_map/product/pallas_call | solution.py:161
  261.1 3.2 collective-permute-start.31
  264.4 11.7 %collective-permute-done.30.refs_0_ = f32[16,64,128]{2,1,0:T(8,128)} collective-permute-done((f32[16,64,128]{2,1,0:T(8,128)}, f32[16,64,128]{2,1,0:T(8,128)}, u32[]{:S(2)}, u32[]{:S(2)}) %collective-permute-start.30) | collective-permute-done | bytes 524320 | tf_op jit(solution)/shard_map/ppermute | solution.py:26
  277.5 3.4 pack.13
  280.9 4.3 %all-to-all-start.2 = ((f32[4,16,64,128]{3,2,1,0:T(8,128)}), f32[4,16,64,128]{3,2,1,0:T(8,128)S(1)}, u32[]{:S(2)}, u32[]{:S(2)}) async-start(f32[4,16,64,128]{3,2,1,0:T(8,128)} %pack.13), calls=%async_computation.2 | async-start | bytes 4194304 | tf_op jit(solution)/shard_map/all_to_all | solution.py:35
  285.2 3.2 collective-permute-start.33
  290.2 8.3 %collective-permute-done.33.refs_1_ = f32[16,64,128]{2,1,0:T(8,128)S(1)} collective-permute-done((f32[16,64,128]{2,1,0:T(8,128)S(1)}, f32[16,64,128]{2,1,0:T(8,128)S(1)}, u32[]{:S(2)}, u32[]{:S(2)}) %collective-permute-start.33) | collective-permute-done | bytes 524320 | tf_op jit(solution)/shard_map/ppermute | solution.py:26
  298.4 3.7 collective-permute-start.38
  303.1 8.1 %collective-permute-done.38.refs_1_ = f32[16,64,128]{2,1,0:T(8,128)S(1)} collective-permute-done((f32[16,64,128]{2,1,0:T(8,128)S(1)}, f32[16,64,128]{2,1,0:T(8,128)S(1)}, u32[]{:S(2)}, u32[]{:S(2)}) %collective-permute-start.38) | collective-permute-done | bytes 524320 | tf_op jit(solution)/shard_map/ppermute | solution.py:26
  311.2 4.1 collective-permute-done.39.refs_2_
  315.3 4.0 pack.15
  320.7 5.3 %all-to-all-start.3 = ((f32[4,24,64,128]{3,2,1,0:T(8,128)}), f32[4,24,64,128]{3,2,1,0:T(8,128)S(1)}, u32[]{:S(2)}, u32[]{:S(2)}) async-start(f32[4,24,64,128]{3,2,1,0:T(8,128)} %pack.15), calls=%async_computation.3 | async-start | bytes 6291456 | tf_op jit(solution)/shard_map/all_to_all | solution.py:35
  326.0 2.8 pack.12
  330.9 2.6 collective-permute-start.28
  333.5 3.4 pack.14
  336.9 2.9 collective-permute-start.35
  339.8 35.7 %collective-permute-done.27.refs_1_ = f32[8,64,128]{2,1,0:T(8,128)S(1)} collective-permute-done((f32[8,64,128]{2,1,0:T(8,128)}, f32[8,64,128]{2,1,0:T(8,128)S(1)}, u32[]{:S(2)}, u32[]{:S(2)}) %collective-permute-start.27) | collective-permute-done | bytes 262176 | tf_op jit(solution)/shard_map/ppermute | solution.py:26
  377.3 15.9 %collective-permute-done.29.refs_3_ = f32[8,64,128]{2,1,0:T(8,128)} collective-permute-done((f32[8,64,128]{2,1,0:T(8,128)}, f32[8,64,128]{2,1,0:T(8,128)}, u32[]{:S(2)}, u32[]{:S(2)}) %collective-permute-start.29) | collective-permute-done | bytes 262176 | tf_op jit(solution)/shard_map/ppermute | solution.py:26
  394.2 5.9 %early.3.refs_2_ = bf16[4,40,64,256]{3,2,1,0:T(8,128)(2,1)} custom-call(s32[4]{0:T(128)} %pad_add_fusion.7.meta, f32[8,64,128]{2,1,0:T(8,128)} %get-tuple-element.29.refs_0_, f32[8,64,128]{2,1,0:T(8,128)} %copy-done.18, f32[8,64,128]{2,1,0:T(8,128)} %collective-permute-done.28.refs_2_, f32[8,64,128]{2,1,0:T(8,128)} %collective-permute-done.29.refs_3_, ...), custom_call_target="tpu_custom_call" | custom-call | tf_op jit(solution)/shard_map/early/pallas_call | solution.py:102
  401.8 13.9 %product.3 = f32[2,8,64,128]{3,2,1,0:T(8,128)} custom-call(s32[4]{0:T(128)} %pad_add_fusion.7.meta, s32[768]{0:T(1024)} %get-tuple-element.44.pos, f32[4,8,64,768]{3,2,1,0:T(8,128)} %pad_maximum_fusion.refs_0_, f32[4,8,64,768]{3,2,1,0:T(8,128)} %collective-permute-done.4.refs_1_, bf16[4,40,64,256]{3,2,1,0:T(8,128)(2,1)} %early.3.refs_2_, ...), custom_call_target="tpu_custom_call" | custom-call | tf_op jit(solution)/shard_map/product/pallas_call | solution.py:161
  (138 shorter events, 44.0 us)
Async XLA Ops:
  6.1 56.2 %copy-start.4 = (f32[8,64,768]{2,1,0:T(8,128)S(1)}, f32[8,64,768]{2,1,0:T(8,128)}, u32[]{:S(2)}) copy-start(f32[8,64,768]{2,1,0:T(8,128)} %turn.3) | copy-start | bytes 4718596
  6.1 36.3 %collective-permute-start.8 = (f32[8,64,768]{2,1,0:T(8,128)}, f32[8,64,768]{2,1,0:T(8,128)S(1)}, u32[]{:S(2)}, u32[]{:S(2)}) collective-permute-start(f32[8,64,768]{2,1,0:T(8,128)} %turn.3), channel_id=1, source_target_pairs={{0,1},{1,2},{2,3},{3,0},{4,5},{5,6},{6,7},{7,4},{8,9},{9,10},{10,1... | collective-permute-start | bytes 4718600 | tf_op jit(solution)/shard_map/ppermute | solution.py:30
  7.4 36.5 %collective-permute-start.9 = (f32[8,64,768]{2,1,0:T(8,128)}, f32[8,64,768]{2,1,0:T(8,128)S(1)}, u32[]{:S(2)}, u32[]{:S(2)}) collective-permute-start(f32[8,64,768]{2,1,0:T(8,128)} %turn.3), channel_id=1, source_target_pairs={{0,3},{1,0},{2,1},{3,2},{4,7},{5,4},{6,5},{7,6},{8,11},{9,8},{10,9... | collective-permute-start | bytes 4718600 | tf_op jit(solution)/shard_map/ppermute | solution.py:30
  42.5 18.5 %collective-permute-start.10 = (f32[4,64,768]{2,1,0:T(8,128)S(1)}, f32[4,64,768]{2,1,0:T(8,128)S(1)}, u32[]{:S(2)}, u32[]{:S(2)}) collective-permute-start(f32[4,64,768]{2,1,0:T(8,128)S(1)} %slice.78), channel_id=1, source_target_pairs={{0,1},{1,2},{2,3},{3,0},{4,5},{5,6},{6,7},{7,4},{8,9},{9,10},{10,1... | collective-permute-start | bytes 2359304 | tf_op jit(solution)/shard_map/ppermute | solution.py:30
  44.0 18.2 %collective-permute-start.11 = (f32[4,64,768]{2,1,0:T(8,128)S(1)}, f32[4,64,768]{2,1,0:T(8,128)S(1)}, u32[]{:S(2)}, u32[]{:S(2)}) collective-permute-start(f32[4,64,768]{2,1,0:T(8,128)S(1)} %slice.79), channel_id=1, source_target_pairs={{0,3},{1,0},{2,1},{3,2},{4,7},{5,4},{6,5},{7,6},{8,11},{9,8},{10,9... | collective-permute-start | bytes 2359304 | tf_op jit(solution)/shard_map/ppermute | solution.py:30
  62.3 32.5 %copy-start.19 = (s32[8,48]{1,0:T(8,128)S(1)}, s32[8,48]{1,0:T(8,128)}, u32[]{:S(2)}) copy-start(s32[8,48]{1,0:T(8,128)} %param.12) | copy-start | bytes 4612
  65.4 180.2 %collective-permute-start.12 = (f32[4,8,64,768]{3,2,1,0:T(8,128)}, f32[4,8,64,768]{3,2,1,0:T(8,128)}, u32[]{:S(2)}, u32[]{:S(2)}) collective-permute-start(f32[4,8,64,768]{3,2,1,0:T(8,128)} %pad_maximum_fusion.1.refs_0_), channel_id=1, source_target_pairs={{0,4},{4,0},{8,12},{12,8},{16,20},{20,16},{24,28},{28,24},{32,36},... | collective-permute-start | bytes 18874376 | tf_op jit(solution)/shard_map/ppermute | solution.py:26
  65.4 10.7 %collective-permute-start.13 = (f32[512,128]{1,0:T(8,128)S(1)}, f32[512,128]{1,0:T(8,128)S(1)}, u32[]{:S(2)}, u32[]{:S(2)}) collective-permute-start(f32[512,128]{1,0:T(8,128)S(1)} %get-tuple-element.40), channel_id=1, source_target_pairs={{0,4},{4,0},{8,12},{12,8},{16,20},{20,16},{24,28},{28,24},{32,36},... | collective-permute-start | bytes 786440 | tf_op jit(solution)/shard_map/ppermute | solution.py:26
  76.1 36.8 %copy-start.5 = (f32[1024,128]{1,0:T(8,128)}, f32[1024,128]{1,0:T(8,128)S(1)}, u32[]{:S(2)}) copy-start(f32[1024,128]{1,0:T(8,128)S(1)} %pad_maximum_fusion.2) | copy-start | bytes 1572868
  76.1 18.2 %collective-permute-start.17 = (f32[16,64,128]{2,1,0:T(8,128)S(1)}, f32[16,64,128]{2,1,0:T(8,128)S(1)}, u32[]{:S(2)}, u32[]{:S(2)}) collective-permute-start(f32[16,64,128]{2,1,0:T(8,128)S(1)} %bitcast.24), channel_id=1, source_target_pairs={{0,32},{4,36},{8,40},{12,44},{16,48},{20,52},{24,56},{28,60},{32,6... | collective-permute-start | bytes 1572872 | tf_op jit(solution)/shard_map/ppermute | solution.py:26
  78.1 23.1 %collective-permute-start.18 = (f32[16,64,128]{2,1,0:T(8,128)S(1)}, f32[16,64,128]{2,1,0:T(8,128)}, u32[]{:S(2)}, u32[]{:S(2)}) collective-permute-start(f32[16,64,128]{2,1,0:T(8,128)S(1)} %bitcast.25), channel_id=1, source_target_pairs={{0,224},{4,228},{8,232},{12,236},{16,240},{20,244},{24,248},{28,25... | collective-permute-start | bytes 1572872 | tf_op jit(solution)/shard_map/ppermute | solution.py:26
  94.3 14.6 %collective-permute-start.19 = (f32[16,64,128]{2,1,0:T(8,128)S(1)}, f32[16,64,128]{2,1,0:T(8,128)S(1)}, u32[]{:S(2)}, u32[]{:S(2)}) collective-permute-start(f32[16,64,128]{2,1,0:T(8,128)S(1)} %collective-permute-done.17.refs_0_), channel_id=1, source_target_pairs={{0,32},{4,36},{8,40},{12,44},{16,48},{20,52},{24,56},{28,60},{32,6... | collective-permute-start | bytes 1572872 | tf_op jit(solution)/shard_map/ppermute | solution.py:26
  94.8 1.3 collective-permute-start
  96.1 4.1 collective-permute-start.5
  98.9 6.2 %collective-permute-start.6 = (s32[4,128]{1,0:T(4,128)S(1)}, s32[4,128]{1,0:T(4,128)S(1)}, u32[]{:S(2)}, u32[]{:S(2)}) collective-permute-start(s32[4,128]{1,0:T(4,128)S(1)} %pad_add_fusion.6), channel_id=1, source_target_pairs={{0,16},{4,20},{8,24},{12,28},{16,0},{20,4},{24,8},{28,12},{32,48},... | collective-permute-start | bytes 6152 | tf_op jit(solution)/shard_map/ppermute | solution.py:26
  100.3 5.0 %collective-permute-start.7 = (s32[4,128]{1,0:T(4,128)S(1)}, s32[4,128]{1,0:T(4,128)S(1)}, u32[]{:S(2)}, u32[]{:S(2)}) collective-permute-start(s32[4,128]{1,0:T(4,128)S(1)} %pad_add_fusion.6), channel_id=1, source_target_pairs={{0,8},{4,12},{8,16},{12,20},{16,24},{20,28},{24,0},{28,4},{32,40},... | collective-permute-start | bytes 6152 | tf_op jit(solution)/shard_map/ppermute | solution.py:26
  101.3 25.0 %collective-permute-start.20 = (f32[16,64,128]{2,1,0:T(8,128)}, f32[16,64,128]{2,1,0:T(8,128)S(1)}, u32[]{:S(2)}, u32[]{:S(2)}) collective-permute-start(f32[16,64,128]{2,1,0:T(8,128)} %collective-permute-done.18.refs_1_), channel_id=1, source_target_pairs={{0,224},{4,228},{8,232},{12,236},{16,240},{20,244},{24,248},{28,25... | collective-permute-start | bytes 1572872 | tf_op jit(solution)/shard_map/ppermute | solution.py:26
  108.9 19.6 %collective-permute-start.24 = (f32[16,64,128]{2,1,0:T(8,128)S(1)}, f32[16,64,128]{2,1,0:T(8,128)}, u32[]{:S(2)}, u32[]{:S(2)}) collective-permute-start(f32[16,64,128]{2,1,0:T(8,128)S(1)} %collective-permute-done.19.refs_0_), channel_id=1, source_target_pairs={{0,32},{4,36},{8,40},{12,44},{16,48},{20,52},{24,56},{28,60},{32,6... | collective-permute-start | bytes 1572872 | tf_op jit(solution)/shard_map/ppermute | solution.py:26
  113.0 44.1 %all-to-all-start = ((f32[4,16,64,128]{3,2,1,0:T(8,128)}), f32[4,16,64,128]{3,2,1,0:T(8,128)S(1)}, u32[]{:S(2)}, u32[]{:S(2)}) async-start(f32[4,16,64,128]{3,2,1,0:T(8,128)} %pack.9), calls=%async_computation | async-start | bytes 4194304 | tf_op jit(solution)/shard_map/all_to_all | solution.py:35
  123.3 39.3 %collective-permute-start.1 = (f32[8,64,768]{2,1,0:T(8,128)}, f32[8,64,768]{2,1,0:T(8,128)}, u32[]{:S(2)}, u32[]{:S(2)}) collective-permute-start(f32[8,64,768]{2,1,0:T(8,128)} %turn.2), channel_id=1, source_target_pairs={{0,1},{1,2},{2,3},{3,0},{4,5},{5,6},{6,7},{7,4},{8,9},{9,10},{10,1... | collective-permute-start | bytes 4718600 | tf_op jit(solution)/shard_map/ppermute | solution.py:30
  126.3 37.6 %collective-permute-start.2 = (f32[8,64,768]{2,1,0:T(8,128)}, f32[8,64,768]{2,1,0:T(8,128)}, u32[]{:S(2)}, u32[]{:S(2)}) collective-permute-start(f32[8,64,768]{2,1,0:T(8,128)} %turn.2), channel_id=1, source_target_pairs={{0,3},{1,0},{2,1},{3,2},{4,7},{5,4},{6,5},{7,6},{8,11},{9,8},{10,9... | collective-permute-start | bytes 4718600 | tf_op jit(solution)/shard_map/ppermute | solution.py:30
  126.3 66.3 %collective-permute-start.3 = (f32[8,64,768]{2,1,0:T(8,128)}, f32[8,64,768]{2,1,0:T(8,128)}, u32[]{:S(2)}, u32[]{:S(2)}) collective-permute-start(f32[8,64,768]{2,1,0:T(8,128)} %turn.2), channel_id=1, source_target_pairs={{0,2},{1,3},{2,0},{3,1},{4,6},{5,7},{6,4},{7,5},{8,10},{9,11},{10,... | collective-permute-start | bytes 4718600 | tf_op jit(solution)/shard_map/ppermute | solution.py:30
  128.5 12.0 %collective-permute-start.25 = (f32[16,64,128]{2,1,0:T(8,128)S(1)}, f32[16,64,128]{2,1,0:T(8,128)S(1)}, u32[]{:S(2)}, u32[]{:S(2)}) collective-permute-start(f32[16,64,128]{2,1,0:T(8,128)S(1)} %collective-permute-done.20.refs_1_), channel_id=1, source_target_pairs={{0,224},{4,228},{8,232},{12,236},{16,240},{20,244},{24,248},{28,25... | collective-permute-start | bytes 1572872 | tf_op jit(solution)/shard_map/ppermute | solution.py:26
  140.5 12.7 %collective-permute-start.26 = (f32[16,64,128]{2,1,0:T(8,128)}, f32[16,64,128]{2,1,0:T(8,128)}, u32[]{:S(2)}, u32[]{:S(2)}) collective-permute-start(f32[16,64,128]{2,1,0:T(8,128)} %collective-permute-done.24.refs_0_), channel_id=1, source_target_pairs={{0,32},{4,36},{8,40},{12,44},{16,48},{20,52},{24,56},{28,60},{32,6... | collective-permute-start | bytes 1572872 | tf_op jit(solution)/shard_map/ppermute | solution.py:26
  158.4 87.2 %all-to-all-start.1 = ((f32[4,24,64,128]{3,2,1,0:T(8,128)}), f32[4,24,64,128]{3,2,1,0:T(8,128)S(1)}, u32[]{:S(2)}, u32[]{:S(2)}) async-start(f32[4,24,64,128]{3,2,1,0:T(8,128)} %pack.11), calls=%async_computation.1 | async-start | bytes 6291456 | tf_op jit(solution)/shard_map/all_to_all | solution.py:35
  197.3 202.8 %collective-permute-start.4 = (f32[4,8,64,768]{3,2,1,0:T(8,128)}, f32[4,8,64,768]{3,2,1,0:T(8,128)}, u32[]{:S(2)}, u32[]{:S(2)}) collective-permute-start(f32[4,8,64,768]{3,2,1,0:T(8,128)} %pad_maximum_fusion.refs_0_), channel_id=1, source_target_pairs={{0,4},{4,0},{8,12},{12,8},{16,20},{20,16},{24,28},{28,24},{32,36},... | collective-permute-start | bytes 18874376 | tf_op jit(solution)/shard_map/ppermute | solution.py:26
  200.1 10.1 %collective-permute-start.14 = (f32[8,64,128]{2,1,0:T(8,128)}, f32[8,64,128]{2,1,0:T(8,128)S(1)}, u32[]{:S(2)}, u32[]{:S(2)}) collective-permute-start(f32[8,64,128]{2,1,0:T(8,128)} %get-tuple-element.22), channel_id=1, source_target_pairs={{0,8},{4,12},{8,16},{12,20},{16,24},{20,28},{24,0},{28,4},{32,40},... | collective-permute-start | bytes 786440 | tf_op jit(solution)/shard_map/ppermute | solution.py:26
  201.8 15.8 %collective-permute-start.15 = (f32[8,64,128]{2,1,0:T(8,128)}, f32[8,64,128]{2,1,0:T(8,128)}, u32[]{:S(2)}, u32[]{:S(2)}) collective-permute-start(f32[8,64,128]{2,1,0:T(8,128)} %get-tuple-element.23), channel_id=1, source_target_pairs={{0,16},{4,20},{8,24},{12,28},{16,0},{20,4},{24,8},{28,12},{32,48},... | collective-permute-start | bytes 786440 | tf_op jit(solution)/shard_map/ppermute | solution.py:26
  204.5 14.0 %collective-permute-start.16 = (f32[8,64,128]{2,1,0:T(8,128)}, f32[8,64,128]{2,1,0:T(8,128)}, u32[]{:S(2)}, u32[]{:S(2)}) collective-permute-start(f32[8,64,128]{2,1,0:T(8,128)} %get-tuple-element.24), channel_id=1, source_target_pairs={{0,24},{4,28},{8,0},{12,4},{16,8},{20,12},{24,16},{28,20},{32,56},... | collective-permute-start | bytes 786440 | tf_op jit(solution)/shard_map/ppermute | solution.py:26
  210.2 18.6 %collective-permute-start.21 = (f32[16,64,128]{2,1,0:T(8,128)}, f32[16,64,128]{2,1,0:T(8,128)}, u32[]{:S(2)}, u32[]{:S(2)}) collective-permute-start(f32[16,64,128]{2,1,0:T(8,128)} %get-tuple-element.26), channel_id=1, source_target_pairs={{0,8},{4,12},{8,16},{12,20},{16,24},{20,28},{24,0},{28,4},{32,40},... | collective-permute-start | bytes 1572872 | tf_op jit(solution)/shard_map/ppermute | solution.py:26
  217.6 22.0 %collective-permute-start.22 = (f32[16,64,128]{2,1,0:T(8,128)}, f32[16,64,128]{2,1,0:T(8,128)}, u32[]{:S(2)}, u32[]{:S(2)}) collective-permute-start(f32[16,64,128]{2,1,0:T(8,128)} %get-tuple-element.27), channel_id=1, source_target_pairs={{0,16},{4,20},{8,24},{12,28},{16,0},{20,4},{24,8},{28,12},{32,48},... | collective-permute-start | bytes 1572872 | tf_op jit(solution)/shard_map/ppermute | solution.py:26
  218.5 21.1 %collective-permute-start.23 = (f32[16,64,128]{2,1,0:T(8,128)}, f32[16,64,128]{2,1,0:T(8,128)}, u32[]{:S(2)}, u32[]{:S(2)}) collective-permute-start(f32[16,64,128]{2,1,0:T(8,128)} %get-tuple-element.28), channel_id=1, source_target_pairs={{0,24},{4,28},{8,0},{12,4},{16,8},{20,12},{24,16},{28,20},{32,56},... | collective-permute-start | bytes 1572872 | tf_op jit(solution)/shard_map/ppermute | solution.py:26
  261.0 15.1 %collective-permute-start.30 = (f32[16,64,128]{2,1,0:T(8,128)}, f32[16,64,128]{2,1,0:T(8,128)}, u32[]{:S(2)}, u32[]{:S(2)}) collective-permute-start(f32[16,64,128]{2,1,0:T(8,128)} %bitcast.21), channel_id=1, source_target_pairs={{0,32},{4,36},{8,40},{12,44},{16,48},{20,52},{24,56},{28,60},{32,6... | collective-permute-start | bytes 1572872 | tf_op jit(solution)/shard_map/ppermute | solution.py:26
  261.1 15.6 %collective-permute-start.31 = (f32[16,64,128]{2,1,0:T(8,128)}, f32[16,64,128]{2,1,0:T(8,128)S(1)}, u32[]{:S(2)}, u32[]{:S(2)}) collective-permute-start(f32[16,64,128]{2,1,0:T(8,128)} %bitcast.22), channel_id=1, source_target_pairs={{0,224},{4,228},{8,232},{12,236},{16,240},{20,244},{24,248},{28,25... | collective-permute-start | bytes 1572872 | tf_op jit(solution)/shard_map/ppermute | solution.py:26
  276.1 14.0 %collective-permute-start.32 = (f32[16,64,128]{2,1,0:T(8,128)}, f32[16,64,128]{2,1,0:T(8,128)S(1)}, u32[]{:S(2)}, u32[]{:S(2)}) collective-permute-start(f32[16,64,128]{2,1,0:T(8,128)} %collective-permute-done.30.refs_0_), channel_id=1, source_target_pairs={{0,32},{4,36},{8,40},{12,44},{16,48},{20,52},{24,56},{28,60},{32,6... | collective-permute-start | bytes 1572872 | tf_op jit(solution)/shard_map/ppermute | solution.py:26
  280.9 38.4 %all-to-all-start.2 = ((f32[4,16,64,128]{3,2,1,0:T(8,128)}), f32[4,16,64,128]{3,2,1,0:T(8,128)S(1)}, u32[]{:S(2)}, u32[]{:S(2)}) async-start(f32[4,16,64,128]{3,2,1,0:T(8,128)} %pack.13), calls=%async_computation.2 | async-start | bytes 4194304 | tf_op jit(solution)/shard_map/all_to_all | solution.py:35
  285.2 13.2 %collective-permute-start.33 = (f32[16,64,128]{2,1,0:T(8,128)S(1)}, f32[16,64,128]{2,1,0:T(8,128)S(1)}, u32[]{:S(2)}, u32[]{:S(2)}) collective-permute-start(f32[16,64,128]{2,1,0:T(8,128)S(1)} %copy-done.13), channel_id=1, source_target_pairs={{0,224},{4,228},{8,232},{12,236},{16,240},{20,244},{24,248},{28,25... | collective-permute-start | bytes 1572872 | tf_op jit(solution)/shard_map/ppermute | solution.py:26
  290.1 13.0 %collective-permute-start.37 = (f32[16,64,128]{2,1,0:T(8,128)S(1)}, f32[16,64,128]{2,1,0:T(8,128)S(1)}, u32[]{:S(2)}, u32[]{:S(2)}) collective-permute-start(f32[16,64,128]{2,1,0:T(8,128)S(1)} %collective-permute-done.32.refs_0_), channel_id=1, source_target_pairs={{0,32},{4,36},{8,40},{12,44},{16,48},{20,52},{24,56},{28,60},{32,6... | collective-permute-start | bytes 1572872 | tf_op jit(solution)/shard_map/ppermute | solution.py:26
  298.4 12.8 %collective-permute-start.38 = (f32[16,64,128]{2,1,0:T(8,128)S(1)}, f32[16,64,128]{2,1,0:T(8,128)S(1)}, u32[]{:S(2)}, u32[]{:S(2)}) collective-permute-start(f32[16,64,128]{2,1,0:T(8,128)S(1)} %collective-permute-done.33.refs_1_), channel_id=1, source_target_pairs={{0,224},{4,228},{8,232},{12,236},{16,240},{20,244},{24,248},{28,25... | collective-permute-start | bytes 1572872 | tf_op jit(solution)/shard_map/ppermute | solution.py:26
  303.1 12.2 %collective-permute-start.39 = (f32[16,64,128]{2,1,0:T(8,128)S(1)}, f32[16,64,128]{2,1,0:T(8,128)}, u32[]{:S(2)}, u32[]{:S(2)}) collective-permute-start(f32[16,64,128]{2,1,0:T(8,128)S(1)} %collective-permute-done.37.refs_0_), channel_id=1, source_target_pairs={{0,32},{4,36},{8,40},{12,44},{16,48},{20,52},{24,56},{28,60},{32,6... | collective-permute-start | bytes 1572872 | tf_op jit(solution)/shard_map/ppermute | solution.py:26
  320.7 79.4 %all-to-all-start.3 = ((f32[4,24,64,128]{3,2,1,0:T(8,128)}), f32[4,24,64,128]{3,2,1,0:T(8,128)S(1)}, u32[]{:S(2)}, u32[]{:S(2)}) async-start(f32[4,24,64,128]{3,2,1,0:T(8,128)} %pack.15), calls=%async_computation.3 | async-start | bytes 6291456 | tf_op jit(solution)/shard_map/all_to_all | solution.py:35
  328.8 46.7 %collective-permute-start.27 = (f32[8,64,128]{2,1,0:T(8,128)}, f32[8,64,128]{2,1,0:T(8,128)S(1)}, u32[]{:S(2)}, u32[]{:S(2)}) collective-permute-start(f32[8,64,128]{2,1,0:T(8,128)} %get-tuple-element.30), channel_id=1, source_target_pairs={{0,8},{4,12},{8,16},{12,20},{16,24},{20,28},{24,0},{28,4},{32,40},... | collective-permute-start | bytes 786440 | tf_op jit(solution)/shard_map/ppermute | solution.py:26
  330.9 45.5 %collective-permute-start.28 = (f32[8,64,128]{2,1,0:T(8,128)}, f32[8,64,128]{2,1,0:T(8,128)}, u32[]{:S(2)}, u32[]{:S(2)}) collective-permute-start(f32[8,64,128]{2,1,0:T(8,128)} %get-tuple-element.31), channel_id=1, source_target_pairs={{0,16},{4,20},{8,24},{12,28},{16,0},{20,4},{24,8},{28,12},{32,48},... | collective-permute-start | bytes 786440 | tf_op jit(solution)/shard_map/ppermute | solution.py:26
  336.9 56.3 %collective-permute-start.34 = (f32[16,64,128]{2,1,0:T(8,128)}, f32[16,64,128]{2,1,0:T(8,128)}, u32[]{:S(2)}, u32[]{:S(2)}) collective-permute-start(f32[16,64,128]{2,1,0:T(8,128)} %get-tuple-element.34), channel_id=1, source_target_pairs={{0,8},{4,12},{8,16},{12,20},{16,24},{20,28},{24,0},{28,4},{32,40},... | collective-permute-start | bytes 1572872 | tf_op jit(solution)/shard_map/ppermute | solution.py:26
  336.9 57.3 %collective-permute-start.35 = (f32[16,64,128]{2,1,0:T(8,128)}, f32[16,64,128]{2,1,0:T(8,128)}, u32[]{:S(2)}, u32[]{:S(2)}) collective-permute-start(f32[16,64,128]{2,1,0:T(8,128)} %get-tuple-element.35), channel_id=1, source_target_pairs={{0,16},{4,20},{8,24},{12,28},{16,0},{20,4},{24,8},{28,12},{32,48},... | collective-permute-start | bytes 1572872 | tf_op jit(solution)/shard_map/ppermute | solution.py:26
  375.6 18.6 %collective-permute-start.36 = (f32[16,64,128]{2,1,0:T(8,128)}, f32[16,64,128]{2,1,0:T(8,128)}, u32[]{:S(2)}, u32[]{:S(2)}) collective-permute-start(f32[16,64,128]{2,1,0:T(8,128)} %get-tuple-element.36), channel_id=1, source_target_pairs={{0,24},{4,28},{8,0},{12,4},{16,8},{20,12},{24,16},{28,20},{32,56},... | collective-permute-start | bytes 1572872 | tf_op jit(solution)/shard_map/ppermute | solution.py:26
  376.4 16.9 %collective-permute-start.29 = (f32[8,64,128]{2,1,0:T(8,128)}, f32[8,64,128]{2,1,0:T(8,128)}, u32[]{:S(2)}, u32[]{:S(2)}) collective-permute-start(f32[8,64,128]{2,1,0:T(8,128)} %get-tuple-element.32), channel_id=1, source_target_pairs={{0,24},{4,28},{8,0},{12,4},{16,8},{20,12},{24,16},{28,20},{32,56},... | collective-permute-start | bytes 786440 | tf_op jit(solution)/shard_map/ppermute | solution.py:26
  416.7 1.6 collective-permute-start.40
  (20 other events, 267.7 us)

commit v3 on v2

--- a/solution.py
+++ b/solution.py
@@ -116,8 +116,11 @@
     )(meta, *arrived)
 
 
-def product_kernel(meta, pos, *refs):
-    early, arrived, out, slabs, split, early_sems, sems = refs[2:]
+def product_kernel(ahead, meta, pos, *refs):
+    if ahead:
+        fetch, refs = refs[0], refs[1:]
+    early, arrived, out = refs[2:5]
+    slabs, split, early_sems, sems = refs[5 + NX * ahead : 9 + NX * ahead]
     y = meta[3]
     step = pl.program_id(0)
 
@@ -152,32 +155,49 @@
                 jnp.concatenate([high, low], axis=0), right, preferred_element_type=jnp.float32
             )
         upper, lower = total[:B], total[B:]
-        out[l, 0] = upper[:, :HALF] + (upper[:, HALF:] + (lower[:, :HALF] + lower[:, HALF:]))
-
-
-def product(meta, pos, own_blocks, partner_blocks, early, arrived):
+        row_sum = upper[:, :HALF] + (upper[:, HALF:] + (lower[:, :HALF] + lower[:, HALF:]))
+        out[l, 0] = row_sum
+        if ahead:
+            refs[-1][l * 8 + step] = row_sum
+    if ahead:
+        @pl.when(step == 7)
+        def _():
+            z, x, c = meta[0], meta[1], meta[2]
+            base = (z * NX + x) * 4
+            for s in range(NX):
+                for j in range(8):
+                    cc, l, f = j >> 2, (j >> 1) & 1, j & 1
+                    row = cc * 8 + fetch[s * 2 + l, base + (c ^ cc) * 2 + f]
+                    refs[5 + s][j] = refs[-1][row]
+
+
+def product(meta, pos, own_blocks, partner_blocks, early, arrived, next_fetch=None):
+    ahead = next_fetch is not None
     block = pl.BlockSpec((4, 1, B, 768), lambda i, *_: (0, i, 0, 0))
     anywhere = pl.BlockSpec(memory_space=pl.ANY)
+    packed = jax.ShapeDtypeStruct((8, B, HALF), jnp.float32)
     return pl.pallas_call(
-        product_kernel,
-        out_shape=jax.ShapeDtypeStruct((2, 8, B, HALF), jnp.float32),
+        functools.partial(product_kernel, int(ahead)),
+        out_shape=[jax.ShapeDtypeStruct((2, 8, B, HALF), jnp.float32)] + [packed] * (NX * ahead),
         grid_spec=pltpu.PrefetchScalarGridSpec(
-            num_scalar_prefetch=2,
+            num_scalar_prefetch=2 + ahead,
             grid=(8,),
             in_specs=[block] * 2 + [anywhere] * 2,
-            out_specs=pl.BlockSpec((2, 1, B, HALF), lambda i, *_: (0, i, 0, 0)),
+            out_specs=[pl.BlockSpec((2, 1, B, HALF), lambda i, *_: (0, i, 0, 0))]
+            + [pl.BlockSpec((8, B, HALF), lambda i, *_: (0, 0, 0))] * (NX * ahead),
             scratch_shapes=[
                 pltpu.VMEM((NX * LATE, B, HALF), jnp.float32),
                 pltpu.VMEM((256, B, 2 * HALF), jnp.bfloat16),
                 pltpu.SemaphoreType.DMA((NX,)),
                 pltpu.SemaphoreType.DMA((NX,)),
-            ],
+            ]
+            + [pltpu.VMEM((16, B, HALF), jnp.float32)] * ahead,
         ),
         name="product",
-    )(meta, pos, own_blocks, partner_blocks, early, arrived)
-
-
-def fetch_rows(own, meta, fetch_x):
+    )(meta, pos, *([next_fetch] if ahead else []), own_blocks, partner_blocks, early, arrived)
+
+
+def fetch_rows(own, meta, fetch_x, ready):
     line = {0: own}
     up = down = own
     for n in range(1, 4):
@@ -187,7 +207,10 @@
     line[4] = rows_shift(up, dz=1)
     arrived = []
     for g, offsets in enumerate(GROUPS):
-        packed = pack(offsets, WHOLE[g], meta, fetch_x, [line[off] for off in offsets])
+        if g == 0 and ready:
+            packed = ready
+        else:
+            packed = pack(offsets, WHOLE[g], meta, fetch_x, [line[off] for off in offsets])
         if WHOLE[g]:
             arrived.append(x_exchange(packed[0]))
             continue
@@ -258,13 +281,15 @@
 
     blocks = [gather_blocks(h_blocks, True), gather_blocks(p_blocks, False)]
 
+    ready = None
+    fetch_x = [jnp.concatenate([a[n::2] for a in along], axis=0) for n in range(2)]
     for n in range(2):
-        fetch_x = jnp.concatenate([a[n::2] for a in along], axis=0)
         low = 2 + 8 * n
         pos = positions(jnp.concatenate([numbers[low : low + 8, :48], other[low : low + 8, :48]], axis=0), z, c)
-        arrived = fetch_rows(own, meta, fetch_x)
+        arrived = fetch_rows(own, meta, fetch_x[n], ready)
         early = early_product(meta, arrived[:-1])
-        own = product(meta, pos, *with_partner(blocks[n]), early, arrived[-1]).reshape(16, B, HALF)
+        own, *ready = product(meta, pos, *with_partner(blocks[n]), early, arrived[-1], fetch_x[1] if n == 0 else None)
+        own = own.reshape(16, B, HALF)
 
     result = own.reshape(2, 512, HALF)
     back = rows_shift(result[1], dc=1)

time: 426 us -> 426 us (level)
    pallas_call x8 -> x7, Pallas kernels: 27.1 us -> 24.3 us  [pack(): pl.pallas_call(functools.partial(pack_kernel, offsets, whole), out_shape=...]
  transfers between devices with their start and end apart: 45 -> 45, of which waited for: 28 -> 29; matrix products, arithmetic and copies ran while one was open for 2% -> 2% of each run, Pallas kernels for 14% -> 13%
where the time goes in v3:
time: 426 us; the launch traced here: 420 us
  waiting for transfers between devices  249 us (58%)
  Pallas kernels  76.5 us (18%)
  starting transfers between devices  73.3 us (17%)
  other arithmetic  11.3 us (3%)
  local copies, waits for them, and re-layouts  8.86 us (2%)
    ppermute x34, waiting for transfers between devices, rows_shift(): return lax.ppermute(array, 'rows', pairs)  168 us
    ppermute x7, waiting for transfers between devices, cols_shift(): return lax.ppermute(array, 'cols', [(y, (y + dy) % NY) for y in range(NY)])  81.6 us
    ppermute x34, starting transfers between devices, rows_shift(): return lax.ppermute(array, 'rows', pairs)  45.8 us
    pallas_call x2, Pallas kernels, product(): pl.pallas_call(functools.partial(product_kernel, int(ahead)), out_shape=[...  28.3 us
    pallas_call x7, Pallas kernels, pack(): pl.pallas_call(functools.partial(pack_kernel, offsets, whole), out_shape=...  24.3 us
    all_to_all x4, starting transfers between devices, x_exchange(): lax.all_to_all(array, 'rows', 0, 0, axis_index_groups=groups, tiled=True)  18.2 us
    pallas_call x2, Pallas kernels, gather_blocks(): pl.pallas_call(turn_kernel, out_shape=jax.ShapeDtypeStruct((8, B, 768), j...  12.2 us
    pallas_call x2, Pallas kernels, early_product(): pl.pallas_call(early_kernel, out_shape=jax.ShapeDtypeStruct((NX, EARLY, B...  11.7 us
  transfers between devices with their start and end apart: 45, of which 29 were waited for; matrix products, arithmetic and copies ran while one was open for 2% of the time, Pallas kernels for 13%

profile of v3, /device:TPU:16, one launch (start us, length us, event | category | flops | bytes accessed | tf_op | source)
XLA Modules:
  0.0 419.7 jit_solution(8906798242477637005)
XLA Ops:
  0.0 6.1 %turn.3 = f32[8,64,768]{2,1,0:T(8,128)} custom-call(f32[8,12,64,64]{3,2,1,0:T(8,128)} %blocks.3), custom_call_target="tpu_custom_call" | custom-call | tf_op jit(solution)/shard_map/turn/pallas_call | solution.py:229
  8.1 34.3 %collective-permute-done.8 = f32[8,64,768]{2,1,0:T(8,128)S(1)} collective-permute-done((f32[8,64,768]{2,1,0:T(8,128)}, f32[8,64,768]{2,1,0:T(8,128)S(1)}, u32[]{:S(2)}, u32[]{:S(2)}) %collective-permute-start.8) | collective-permute-done | bytes 1572896 | tf_op jit(solution)/shard_map/ppermute | solution.py:30
  44.8 16.3 %collective-permute-done.10 = f32[4,64,768]{2,1,0:T(8,128)S(1)} collective-permute-done((f32[4,64,768]{2,1,0:T(8,128)S(1)}, f32[4,64,768]{2,1,0:T(8,128)S(1)}, u32[]{:S(2)}, u32[]{:S(2)}) %collective-permute-start.10) | collective-permute-done | bytes 786464 | tf_op jit(solution)/shard_map/ppermute | solution.py:30
  62.4 3.0 pad_maximum_fusion.1.refs_1_
  66.0 10.1 %collective-permute-done.13 = f32[512,128]{1,0:T(8,128)S(1)} collective-permute-done((f32[512,128]{1,0:T(8,128)S(1)}, f32[512,128]{1,0:T(8,128)S(1)}, u32[]{:S(2)}, u32[]{:S(2)}) %collective-permute-start.13) | collective-permute-done | bytes 262176 | tf_op jit(solution)/shard_map/ppermute | solution.py:26
  78.1 4.0 collective-permute-start.18
  82.2 12.1 %collective-permute-done.17.refs_0_ = f32[16,64,128]{2,1,0:T(8,128)S(1)} collective-permute-done((f32[16,64,128]{2,1,0:T(8,128)S(1)}, f32[16,64,128]{2,1,0:T(8,128)S(1)}, u32[]{:S(2)}, u32[]{:S(2)}) %collective-permute-start.17) | collective-permute-done | bytes 524320 | tf_op jit(solution)/shard_map/ppermute | solution.py:26
  96.1 3.2 collective-permute-start.20
  99.3 2.8 collective-permute-start.5
  109.6 3.4 pack.8
  113.0 4.3 %all-to-all-start = ((f32[4,16,64,128]{3,2,1,0:T(8,128)}), f32[4,16,64,128]{3,2,1,0:T(8,128)S(1)}, u32[]{:S(2)}, u32[]{:S(2)}) async-start(f32[4,16,64,128]{3,2,1,0:T(8,128)} %pack.8), calls=%async_computation | async-start | bytes 4194304 | tf_op jit(solution)/shard_map/all_to_all | solution.py:35
  117.2 6.1 %turn.2 = f32[8,64,768]{2,1,0:T(8,128)} custom-call(f32[8,12,64,64]{3,2,1,0:T(8,128)} %blocks.2), custom_call_target="tpu_custom_call" | custom-call | tf_op jit(solution)/shard_map/turn/pallas_call | solution.py:229
  123.3 2.9 collective-permute-start.1
  126.3 2.2 collective-permute-start.3
  128.5 3.2 collective-permute-start.25
  131.7 8.8 %collective-permute-done.25.refs_1_ = f32[16,64,128]{2,1,0:T(8,128)S(1)} collective-permute-done((f32[16,64,128]{2,1,0:T(8,128)S(1)}, f32[16,64,128]{2,1,0:T(8,128)S(1)}, u32[]{:S(2)}, u32[]{:S(2)}) %collective-permute-start.25) | collective-permute-done | bytes 524320 | tf_op jit(solution)/shard_map/ppermute | solution.py:26
  140.5 12.7 %collective-permute-done.26.refs_2_ = f32[16,64,128]{2,1,0:T(8,128)} collective-permute-done((f32[16,64,128]{2,1,0:T(8,128)}, f32[16,64,128]{2,1,0:T(8,128)}, u32[]{:S(2)}, u32[]{:S(2)}) %collective-permute-start.26) | collective-permute-done | bytes 524320 | tf_op jit(solution)/shard_map/ppermute | solution.py:26
  153.1 3.9 pack.10
  158.4 4.2 %all-to-all-start.1 = ((f32[4,24,64,128]{3,2,1,0:T(8,128)}), f32[4,24,64,128]{3,2,1,0:T(8,128)S(1)}, u32[]{:S(2)}, u32[]{:S(2)}) async-start(f32[4,24,64,128]{3,2,1,0:T(8,128)} %pack.10), calls=%async_computation.1 | async-start | bytes 6291456 | tf_op jit(solution)/shard_map/all_to_all | solution.py:35
  163.8 28.7 %collective-permute-done.3 = f32[8,64,768]{2,1,0:T(8,128)} collective-permute-done((f32[8,64,768]{2,1,0:T(8,128)}, f32[8,64,768]{2,1,0:T(8,128)}, u32[]{:S(2)}, u32[]{:S(2)}) %collective-permute-start.3) | collective-permute-done | bytes 1572896 | tf_op jit(solution)/shard_map/ppermute | solution.py:30
  192.5 4.8 %pad_maximum_fusion.refs_0_ = f32[4,8,64,768]{3,2,1,0:T(8,128)} fusion(f32[1,8,64,768]{3,2,1,0:T(8,128)} %bitcast.7, f32[1,8,64,768]{3,2,1,0:T(8,128)} %bitcast.6, f32[1,8,64,768]{3,2,1,0:T(8,128)} %bitcast.5, f32[1,8,64,768]{3,2,1,0:T(8,128)} %bitcast.17), kind=kLoop, calls=%fused_computation | loop fusion | flops 4718592 | bytes 12582912 | tf_op jit(solution)/shard_map/stack | solution.py:249
  197.3 2.8 pack.7
  201.8 2.7 collective-permute-start.15
  206.1 3.4 pack.9
  211.2 6.4 %collective-permute-done.15.refs_2_ = f32[8,64,128]{2,1,0:T(8,128)} collective-permute-done((f32[8,64,128]{2,1,0:T(8,128)}, f32[8,64,128]{2,1,0:T(8,128)}, u32[]{:S(2)}, u32[]{:S(2)}) %collective-permute-start.15) | collective-permute-done | bytes 262176 | tf_op jit(solution)/shard_map/ppermute | solution.py:26
  221.4 7.4 %collective-permute-done.21.refs_6_ = f32[16,64,128]{2,1,0:T(8,128)} collective-permute-done((f32[16,64,128]{2,1,0:T(8,128)}, f32[16,64,128]{2,1,0:T(8,128)}, u32[]{:S(2)}, u32[]{:S(2)}) %collective-permute-start.21) | collective-permute-done | bytes 524320 | tf_op jit(solution)/shard_map/ppermute | solution.py:26
  228.8 10.9 %collective-permute-done.22.refs_7_ = f32[16,64,128]{2,1,0:T(8,128)} collective-permute-done((f32[16,64,128]{2,1,0:T(8,128)}, f32[16,64,128]{2,1,0:T(8,128)}, u32[]{:S(2)}, u32[]{:S(2)}) %collective-permute-start.22) | collective-permute-done | bytes 524320 | tf_op jit(solution)/shard_map/ppermute | solution.py:26
  239.6 5.8 %early.2.refs_3_ = bf16[4,40,64,256]{3,2,1,0:T(8,128)(2,1)} custom-call(s32[4]{0:T(128)} %pad_add_fusion.7.meta, f32[8,64,128]{2,1,0:T(8,128)} %get-tuple-element.22.refs_0_, f32[8,64,128]{2,1,0:T(8,128)} %copy-done.17, f32[8,64,128]{2,1,0:T(8,128)} %collective-permute-done.15.refs_2_, f32[8,64,128]{2,1,0:T(8,128)} %collective-permute-done.16.refs_3_, ...), custom_call_target="tpu_custom_call" | custom-call | tf_op jit(solution)/shard_map/early/pallas_call | solution.py:102
  247.1 14.4 %product.2 = (f32[2,8,64,128]{3,2,1,0:T(8,128)}, f32[8,64,128]{2,1,0:T(8,128)}, f32[8,64,128]{2,1,0:T(8,128)}, f32[8,64,128]{2,1,0:T(8,128)}, f32[8,64,128]{2,1,0:T(8,128)}) custom-call(s32[4]{0:T(128)} %pad_add_fusion.7.meta, s32[768]{0:T(1024)} %get-tuple-element.45.pos, s32[8,128]{1,0:T(8,128)} %pad_add_fusion.4.refs_0_.fetch, ...), custom_call_target="tpu_custom_call" | custom-call | tf_op jit(solution)/shard_map/product/pallas_call | solution.py:179
  261.6 3.2 collective-permute-start.31
  264.9 11.8 %collective-permute-done.30.refs_0_ = f32[16,64,128]{2,1,0:T(8,128)} collective-permute-done((f32[16,64,128]{2,1,0:T(8,128)}, f32[16,64,128]{2,1,0:T(8,128)}, u32[]{:S(2)}, u32[]{:S(2)}) %collective-permute-start.30) | collective-permute-done | bytes 524320 | tf_op jit(solution)/shard_map/ppermute | solution.py:26
  277.4 3.4 pack.11
  280.8 4.3 %all-to-all-start.2 = ((f32[4,16,64,128]{3,2,1,0:T(8,128)}), f32[4,16,64,128]{3,2,1,0:T(8,128)S(1)}, u32[]{:S(2)}, u32[]{:S(2)}) async-start(f32[4,16,64,128]{3,2,1,0:T(8,128)} %pack.11), calls=%async_computation.2 | async-start | bytes 4194304 | tf_op jit(solution)/shard_map/all_to_all | solution.py:35
  285.1 3.2 collective-permute-start.33
  288.4 2.3 collective-permute-done.32.refs_0_
  290.7 7.6 %collective-permute-done.33.refs_1_ = f32[16,64,128]{2,1,0:T(8,128)S(1)} collective-permute-done((f32[16,64,128]{2,1,0:T(8,128)S(1)}, f32[16,64,128]{2,1,0:T(8,128)S(1)}, u32[]{:S(2)}, u32[]{:S(2)}) %collective-permute-start.33) | collective-permute-done | bytes 524320 | tf_op jit(solution)/shard_map/ppermute | solution.py:26
  298.3 3.7 collective-permute-start.38
  303.6 7.5 %collective-permute-done.38.refs_1_ = f32[16,64,128]{2,1,0:T(8,128)S(1)} collective-permute-done((f32[16,64,128]{2,1,0:T(8,128)S(1)}, f32[16,64,128]{2,1,0:T(8,128)S(1)}, u32[]{:S(2)}, u32[]{:S(2)}) %collective-permute-start.38) | collective-permute-done | bytes 524320 | tf_op jit(solution)/shard_map/ppermute | solution.py:26
  311.1 4.8 %collective-permute-done.39.refs_2_ = f32[16,64,128]{2,1,0:T(8,128)} collective-permute-done((f32[16,64,128]{2,1,0:T(8,128)S(1)}, f32[16,64,128]{2,1,0:T(8,128)}, u32[]{:S(2)}, u32[]{:S(2)}) %collective-permute-start.39) | collective-permute-done | bytes 524320 | tf_op jit(solution)/shard_map/ppermute | solution.py:26
  315.9 4.0 pack.13
  321.2 5.3 %all-to-all-start.3 = ((f32[4,24,64,128]{3,2,1,0:T(8,128)}), f32[4,24,64,128]{3,2,1,0:T(8,128)S(1)}, u32[]{:S(2)}, u32[]{:S(2)}) async-start(f32[4,24,64,128]{3,2,1,0:T(8,128)} %pack.13), calls=%async_computation.3 | async-start | bytes 6291456 | tf_op jit(solution)/shard_map/all_to_all | solution.py:35
  328.7 2.5 collective-permute-start.28
  331.2 3.4 pack.12
  334.6 2.9 collective-permute-start.35
  337.5 38.5 %collective-permute-done.27.refs_1_ = f32[8,64,128]{2,1,0:T(8,128)S(1)} collective-permute-done((f32[8,64,128]{2,1,0:T(8,128)}, f32[8,64,128]{2,1,0:T(8,128)S(1)}, u32[]{:S(2)}, u32[]{:S(2)}) %collective-permute-start.27) | collective-permute-done | bytes 262176 | tf_op jit(solution)/shard_map/ppermute | solution.py:26
  377.9 15.9 %collective-permute-done.29.refs_3_ = f32[8,64,128]{2,1,0:T(8,128)} collective-permute-done((f32[8,64,128]{2,1,0:T(8,128)}, f32[8,64,128]{2,1,0:T(8,128)}, u32[]{:S(2)}, u32[]{:S(2)}) %collective-permute-start.29) | collective-permute-done | bytes 262176 | tf_op jit(solution)/shard_map/ppermute | solution.py:26
  394.7 5.9 %early.3.refs_2_ = bf16[4,40,64,256]{3,2,1,0:T(8,128)(2,1)} custom-call(s32[4]{0:T(128)} %pad_add_fusion.7.meta, f32[8,64,128]{2,1,0:T(8,128)} %get-tuple-element.30.refs_0_, f32[8,64,128]{2,1,0:T(8,128)} %copy-done.18, f32[8,64,128]{2,1,0:T(8,128)} %collective-permute-done.28.refs_2_, f32[8,64,128]{2,1,0:T(8,128)} %collective-permute-done.29.refs_3_, ...), custom_call_target="tpu_custom_call" | custom-call | tf_op jit(solution)/shard_map/early/pallas_call | solution.py:102
  402.3 13.9 %product.3 = f32[2,8,64,128]{3,2,1,0:T(8,128)} custom-call(s32[4]{0:T(128)} %pad_add_fusion.7.meta, s32[768]{0:T(1024)} %get-tuple-element.46.pos, f32[4,8,64,768]{3,2,1,0:T(8,128)} %pad_maximum_fusion.refs_0_, f32[4,8,64,768]{3,2,1,0:T(8,128)} %collective-permute-done.4.refs_1_, bf16[4,40,64,256]{3,2,1,0:T(8,128)(2,1)} %early.3.refs_2_, ...), custom_call_target="tpu_custom_call" | custom-call | tf_op jit(solution)/shard_map/product/pallas_call | solution.py:179
  (137 shorter events, 44.4 us)
Async XLA Ops:
  6.1 56.2 %copy-start.4 = (f32[8,64,768]{2,1,0:T(8,128)S(1)}, f32[8,64,768]{2,1,0:T(8,128)}, u32[]{:S(2)}) copy-start(f32[8,64,768]{2,1,0:T(8,128)} %turn.3) | copy-start | bytes 4718596
  6.1 36.3 %collective-permute-start.8 = (f32[8,64,768]{2,1,0:T(8,128)}, f32[8,64,768]{2,1,0:T(8,128)S(1)}, u32[]{:S(2)}, u32[]{:S(2)}) collective-permute-start(f32[8,64,768]{2,1,0:T(8,128)} %turn.3), channel_id=1, source_target_pairs={{0,1},{1,2},{2,3},{3,0},{4,5},{5,6},{6,7},{7,4},{8,9},{9,10},{10,1... | collective-permute-start | bytes 4718600 | tf_op jit(solution)/shard_map/ppermute | solution.py:30
  7.4 36.5 %collective-permute-start.9 = (f32[8,64,768]{2,1,0:T(8,128)}, f32[8,64,768]{2,1,0:T(8,128)S(1)}, u32[]{:S(2)}, u32[]{:S(2)}) collective-permute-start(f32[8,64,768]{2,1,0:T(8,128)} %turn.3), channel_id=1, source_target_pairs={{0,3},{1,0},{2,1},{3,2},{4,7},{5,4},{6,5},{7,6},{8,11},{9,8},{10,9... | collective-permute-start | bytes 4718600 | tf_op jit(solution)/shard_map/ppermute | solution.py:30
  42.5 18.5 %collective-permute-start.10 = (f32[4,64,768]{2,1,0:T(8,128)S(1)}, f32[4,64,768]{2,1,0:T(8,128)S(1)}, u32[]{:S(2)}, u32[]{:S(2)}) collective-permute-start(f32[4,64,768]{2,1,0:T(8,128)S(1)} %slice.78), channel_id=1, source_target_pairs={{0,1},{1,2},{2,3},{3,0},{4,5},{5,6},{6,7},{7,4},{8,9},{9,10},{10,1... | collective-permute-start | bytes 2359304 | tf_op jit(solution)/shard_map/ppermute | solution.py:30
  44.0 18.2 %collective-permute-start.11 = (f32[4,64,768]{2,1,0:T(8,128)S(1)}, f32[4,64,768]{2,1,0:T(8,128)S(1)}, u32[]{:S(2)}, u32[]{:S(2)}) collective-permute-start(f32[4,64,768]{2,1,0:T(8,128)S(1)} %slice.79), channel_id=1, source_target_pairs={{0,3},{1,0},{2,1},{3,2},{4,7},{5,4},{6,5},{7,6},{8,11},{9,8},{10,9... | collective-permute-start | bytes 2359304 | tf_op jit(solution)/shard_map/ppermute | solution.py:30
  62.3 32.5 %copy-start.19 = (s32[8,48]{1,0:T(8,128)S(1)}, s32[8,48]{1,0:T(8,128)}, u32[]{:S(2)}) copy-start(s32[8,48]{1,0:T(8,128)} %param.12) | copy-start | bytes 4612
  65.4 180.2 %collective-permute-start.12 = (f32[4,8,64,768]{3,2,1,0:T(8,128)}, f32[4,8,64,768]{3,2,1,0:T(8,128)}, u32[]{:S(2)}, u32[]{:S(2)}) collective-permute-start(f32[4,8,64,768]{3,2,1,0:T(8,128)} %pad_maximum_fusion.1.refs_1_), channel_id=1, source_target_pairs={{0,4},{4,0},{8,12},{12,8},{16,20},{20,16},{24,28},{28,24},{32,36},... | collective-permute-start | bytes 18874376 | tf_op jit(solution)/shard_map/ppermute | solution.py:26
  65.4 10.7 %collective-permute-start.13 = (f32[512,128]{1,0:T(8,128)S(1)}, f32[512,128]{1,0:T(8,128)S(1)}, u32[]{:S(2)}, u32[]{:S(2)}) collective-permute-start(f32[512,128]{1,0:T(8,128)S(1)} %get-tuple-element.42), channel_id=1, source_target_pairs={{0,4},{4,0},{8,12},{12,8},{16,20},{20,16},{24,28},{28,24},{32,36},... | collective-permute-start | bytes 786440 | tf_op jit(solution)/shard_map/ppermute | solution.py:26
  76.1 36.8 %copy-start.5 = (f32[1024,128]{1,0:T(8,128)}, f32[1024,128]{1,0:T(8,128)S(1)}, u32[]{:S(2)}) copy-start(f32[1024,128]{1,0:T(8,128)S(1)} %pad_maximum_fusion.2) | copy-start | bytes 1572868
  76.1 18.2 %collective-permute-start.17 = (f32[16,64,128]{2,1,0:T(8,128)S(1)}, f32[16,64,128]{2,1,0:T(8,128)S(1)}, u32[]{:S(2)}, u32[]{:S(2)}) collective-permute-start(f32[16,64,128]{2,1,0:T(8,128)S(1)} %bitcast.21), channel_id=1, source_target_pairs={{0,32},{4,36},{8,40},{12,44},{16,48},{20,52},{24,56},{28,60},{32,6... | collective-permute-start | bytes 1572872 | tf_op jit(solution)/shard_map/ppermute | solution.py:26
  78.1 18.0 %collective-permute-start.18 = (f32[16,64,128]{2,1,0:T(8,128)S(1)}, f32[16,64,128]{2,1,0:T(8,128)}, u32[]{:S(2)}, u32[]{:S(2)}) collective-permute-start(f32[16,64,128]{2,1,0:T(8,128)S(1)} %bitcast.22), channel_id=1, source_target_pairs={{0,224},{4,228},{8,232},{12,236},{16,240},{20,244},{24,248},{28,25... | collective-permute-start | bytes 1572872 | tf_op jit(solution)/shard_map/ppermute | solution.py:26
  94.3 14.6 %collective-permute-start.19 = (f32[16,64,128]{2,1,0:T(8,128)S(1)}, f32[16,64,128]{2,1,0:T(8,128)S(1)}, u32[]{:S(2)}, u32[]{:S(2)}) collective-permute-start(f32[16,64,128]{2,1,0:T(8,128)S(1)} %collective-permute-done.17.refs_0_), channel_id=1, source_target_pairs={{0,32},{4,36},{8,40},{12,44},{16,48},{20,52},{24,56},{28,60},{32,6... | collective-permute-start | bytes 1572872 | tf_op jit(solution)/shard_map/ppermute | solution.py:26
  94.8 1.3 collective-permute-start
  96.1 30.2 %collective-permute-start.20 = (f32[16,64,128]{2,1,0:T(8,128)}, f32[16,64,128]{2,1,0:T(8,128)S(1)}, u32[]{:S(2)}, u32[]{:S(2)}) collective-permute-start(f32[16,64,128]{2,1,0:T(8,128)} %collective-permute-done.18.refs_1_), channel_id=1, source_target_pairs={{0,224},{4,228},{8,232},{12,236},{16,240},{20,244},{24,248},{28,25... | collective-permute-start | bytes 1572872 | tf_op jit(solution)/shard_map/ppermute | solution.py:26
  99.3 4.1 collective-permute-start.5
  102.1 5.1 %collective-permute-start.6 = (s32[4,128]{1,0:T(4,128)S(1)}, s32[4,128]{1,0:T(4,128)S(1)}, u32[]{:S(2)}, u32[]{:S(2)}) collective-permute-start(s32[4,128]{1,0:T(4,128)S(1)} %pad_add_fusion.6), channel_id=1, source_target_pairs={{0,16},{4,20},{8,24},{12,28},{16,0},{20,4},{24,8},{28,12},{32,48},... | collective-permute-start | bytes 6152 | tf_op jit(solution)/shard_map/ppermute | solution.py:26
  103.4 5.0 %collective-permute-start.7 = (s32[4,128]{1,0:T(4,128)S(1)}, s32[4,128]{1,0:T(4,128)S(1)}, u32[]{:S(2)}, u32[]{:S(2)}) collective-permute-start(s32[4,128]{1,0:T(4,128)S(1)} %pad_add_fusion.6), channel_id=1, source_target_pairs={{0,8},{4,12},{8,16},{12,20},{16,24},{20,28},{24,0},{28,4},{32,40},... | collective-permute-start | bytes 6152 | tf_op jit(solution)/shard_map/ppermute | solution.py:26
  108.9 19.6 %collective-permute-start.24 = (f32[16,64,128]{2,1,0:T(8,128)S(1)}, f32[16,64,128]{2,1,0:T(8,128)}, u32[]{:S(2)}, u32[]{:S(2)}) collective-permute-start(f32[16,64,128]{2,1,0:T(8,128)S(1)} %collective-permute-done.19.refs_0_), channel_id=1, source_target_pairs={{0,32},{4,36},{8,40},{12,44},{16,48},{20,52},{24,56},{28,60},{32,6... | collective-permute-start | bytes 1572872 | tf_op jit(solution)/shard_map/ppermute | solution.py:26
  113.0 44.1 %all-to-all-start = ((f32[4,16,64,128]{3,2,1,0:T(8,128)}), f32[4,16,64,128]{3,2,1,0:T(8,128)S(1)}, u32[]{:S(2)}, u32[]{:S(2)}) async-start(f32[4,16,64,128]{3,2,1,0:T(8,128)} %pack.8), calls=%async_computation | async-start | bytes 4194304 | tf_op jit(solution)/shard_map/all_to_all | solution.py:35
  123.3 39.3 %collective-permute-start.1 = (f32[8,64,768]{2,1,0:T(8,128)}, f32[8,64,768]{2,1,0:T(8,128)}, u32[]{:S(2)}, u32[]{:S(2)}) collective-permute-start(f32[8,64,768]{2,1,0:T(8,128)} %turn.2), channel_id=1, source_target_pairs={{0,1},{1,2},{2,3},{3,0},{4,5},{5,6},{6,7},{7,4},{8,9},{9,10},{10,1... | collective-permute-start | bytes 4718600 | tf_op jit(solution)/shard_map/ppermute | solution.py:30
  126.3 37.6 %collective-permute-start.2 = (f32[8,64,768]{2,1,0:T(8,128)}, f32[8,64,768]{2,1,0:T(8,128)}, u32[]{:S(2)}, u32[]{:S(2)}) collective-permute-start(f32[8,64,768]{2,1,0:T(8,128)} %turn.2), channel_id=1, source_target_pairs={{0,3},{1,0},{2,1},{3,2},{4,7},{5,4},{6,5},{7,6},{8,11},{9,8},{10,9... | collective-permute-start | bytes 4718600 | tf_op jit(solution)/shard_map/ppermute | solution.py:30
  126.3 66.3 %collective-permute-start.3 = (f32[8,64,768]{2,1,0:T(8,128)}, f32[8,64,768]{2,1,0:T(8,128)}, u32[]{:S(2)}, u32[]{:S(2)}) collective-permute-start(f32[8,64,768]{2,1,0:T(8,128)} %turn.2), channel_id=1, source_target_pairs={{0,2},{1,3},{2,0},{3,1},{4,6},{5,7},{6,4},{7,5},{8,10},{9,11},{10,... | collective-permute-start | bytes 4718600 | tf_op jit(solution)/shard_map/ppermute | solution.py:30
  128.5 12.0 %collective-permute-start.25 = (f32[16,64,128]{2,1,0:T(8,128)S(1)}, f32[16,64,128]{2,1,0:T(8,128)S(1)}, u32[]{:S(2)}, u32[]{:S(2)}) collective-permute-start(f32[16,64,128]{2,1,0:T(8,128)S(1)} %collective-permute-done.20.refs_1_), channel_id=1, source_target_pairs={{0,224},{4,228},{8,232},{12,236},{16,240},{20,244},{24,248},{28,25... | collective-permute-start | bytes 1572872 | tf_op jit(solution)/shard_map/ppermute | solution.py:26
  140.5 12.7 %collective-permute-start.26 = (f32[16,64,128]{2,1,0:T(8,128)}, f32[16,64,128]{2,1,0:T(8,128)}, u32[]{:S(2)}, u32[]{:S(2)}) collective-permute-start(f32[16,64,128]{2,1,0:T(8,128)} %collective-permute-done.24.refs_0_), channel_id=1, source_target_pairs={{0,32},{4,36},{8,40},{12,44},{16,48},{20,52},{24,56},{28,60},{32,6... | collective-permute-start | bytes 1572872 | tf_op jit(solution)/shard_map/ppermute | solution.py:26
  158.4 87.2 %all-to-all-start.1 = ((f32[4,24,64,128]{3,2,1,0:T(8,128)}), f32[4,24,64,128]{3,2,1,0:T(8,128)S(1)}, u32[]{:S(2)}, u32[]{:S(2)}) async-start(f32[4,24,64,128]{3,2,1,0:T(8,128)} %pack.10), calls=%async_computation.1 | async-start | bytes 6291456 | tf_op jit(solution)/shard_map/all_to_all | solution.py:35
  197.3 203.3 %collective-permute-start.4 = (f32[4,8,64,768]{3,2,1,0:T(8,128)}, f32[4,8,64,768]{3,2,1,0:T(8,128)}, u32[]{:S(2)}, u32[]{:S(2)}) collective-permute-start(f32[4,8,64,768]{3,2,1,0:T(8,128)} %pad_maximum_fusion.refs_0_), channel_id=1, source_target_pairs={{0,4},{4,0},{8,12},{12,8},{16,20},{20,16},{24,28},{28,24},{32,36},... | collective-permute-start | bytes 18874376 | tf_op jit(solution)/shard_map/ppermute | solution.py:26
  200.1 10.1 %collective-permute-start.14 = (f32[8,64,128]{2,1,0:T(8,128)}, f32[8,64,128]{2,1,0:T(8,128)S(1)}, u32[]{:S(2)}, u32[]{:S(2)}) collective-permute-start(f32[8,64,128]{2,1,0:T(8,128)} %get-tuple-element.23), channel_id=1, source_target_pairs={{0,8},{4,12},{8,16},{12,20},{16,24},{20,28},{24,0},{28,4},{32,40},... | collective-permute-start | bytes 786440 | tf_op jit(solution)/shard_map/ppermute | solution.py:26
  201.8 15.8 %collective-permute-start.15 = (f32[8,64,128]{2,1,0:T(8,128)}, f32[8,64,128]{2,1,0:T(8,128)}, u32[]{:S(2)}, u32[]{:S(2)}) collective-permute-start(f32[8,64,128]{2,1,0:T(8,128)} %get-tuple-element.24), channel_id=1, source_target_pairs={{0,16},{4,20},{8,24},{12,28},{16,0},{20,4},{24,8},{28,12},{32,48},... | collective-permute-start | bytes 786440 | tf_op jit(solution)/shard_map/ppermute | solution.py:26
  204.5 14.0 %collective-permute-start.16 = (f32[8,64,128]{2,1,0:T(8,128)}, f32[8,64,128]{2,1,0:T(8,128)}, u32[]{:S(2)}, u32[]{:S(2)}) collective-permute-start(f32[8,64,128]{2,1,0:T(8,128)} %get-tuple-element.25), channel_id=1, source_target_pairs={{0,24},{4,28},{8,0},{12,4},{16,8},{20,12},{24,16},{28,20},{32,56},... | collective-permute-start | bytes 786440 | tf_op jit(solution)/shard_map/ppermute | solution.py:26
  210.2 18.6 %collective-permute-start.21 = (f32[16,64,128]{2,1,0:T(8,128)}, f32[16,64,128]{2,1,0:T(8,128)}, u32[]{:S(2)}, u32[]{:S(2)}) collective-permute-start(f32[16,64,128]{2,1,0:T(8,128)} %get-tuple-element.27), channel_id=1, source_target_pairs={{0,8},{4,12},{8,16},{12,20},{16,24},{20,28},{24,0},{28,4},{32,40},... | collective-permute-start | bytes 1572872 | tf_op jit(solution)/shard_map/ppermute | solution.py:26
  217.6 22.0 %collective-permute-start.22 = (f32[16,64,128]{2,1,0:T(8,128)}, f32[16,64,128]{2,1,0:T(8,128)}, u32[]{:S(2)}, u32[]{:S(2)}) collective-permute-start(f32[16,64,128]{2,1,0:T(8,128)} %get-tuple-element.28), channel_id=1, source_target_pairs={{0,16},{4,20},{8,24},{12,28},{16,0},{20,4},{24,8},{28,12},{32,48},... | collective-permute-start | bytes 1572872 | tf_op jit(solution)/shard_map/ppermute | solution.py:26
  218.5 21.1 %collective-permute-start.23 = (f32[16,64,128]{2,1,0:T(8,128)}, f32[16,64,128]{2,1,0:T(8,128)}, u32[]{:S(2)}, u32[]{:S(2)}) collective-permute-start(f32[16,64,128]{2,1,0:T(8,128)} %get-tuple-element.29), channel_id=1, source_target_pairs={{0,24},{4,28},{8,0},{12,4},{16,8},{20,12},{24,16},{28,20},{32,56},... | collective-permute-start | bytes 1572872 | tf_op jit(solution)/shard_map/ppermute | solution.py:26
  261.5 15.1 %collective-permute-start.30 = (f32[16,64,128]{2,1,0:T(8,128)}, f32[16,64,128]{2,1,0:T(8,128)}, u32[]{:S(2)}, u32[]{:S(2)}) collective-permute-start(f32[16,64,128]{2,1,0:T(8,128)} %bitcast.26), channel_id=1, source_target_pairs={{0,32},{4,36},{8,40},{12,44},{16,48},{20,52},{24,56},{28,60},{32,6... | collective-permute-start | bytes 1572872 | tf_op jit(solution)/shard_map/ppermute | solution.py:26
  261.6 15.0 %collective-permute-start.31 = (f32[16,64,128]{2,1,0:T(8,128)}, f32[16,64,128]{2,1,0:T(8,128)S(1)}, u32[]{:S(2)}, u32[]{:S(2)}) collective-permute-start(f32[16,64,128]{2,1,0:T(8,128)} %bitcast.27), channel_id=1, source_target_pairs={{0,224},{4,228},{8,232},{12,236},{16,240},{20,244},{24,248},{28,25... | collective-permute-start | bytes 1572872 | tf_op jit(solution)/shard_map/ppermute | solution.py:26
  276.6 14.0 %collective-permute-start.32 = (f32[16,64,128]{2,1,0:T(8,128)}, f32[16,64,128]{2,1,0:T(8,128)S(1)}, u32[]{:S(2)}, u32[]{:S(2)}) collective-permute-start(f32[16,64,128]{2,1,0:T(8,128)} %collective-permute-done.30.refs_0_), channel_id=1, source_target_pairs={{0,32},{4,36},{8,40},{12,44},{16,48},{20,52},{24,56},{28,60},{32,6... | collective-permute-start | bytes 1572872 | tf_op jit(solution)/shard_map/ppermute | solution.py:26
  280.8 39.0 %all-to-all-start.2 = ((f32[4,16,64,128]{3,2,1,0:T(8,128)}), f32[4,16,64,128]{3,2,1,0:T(8,128)S(1)}, u32[]{:S(2)}, u32[]{:S(2)}) async-start(f32[4,16,64,128]{3,2,1,0:T(8,128)} %pack.11), calls=%async_computation.2 | async-start | bytes 4194304 | tf_op jit(solution)/shard_map/all_to_all | solution.py:35
  285.1 13.2 %collective-permute-start.33 = (f32[16,64,128]{2,1,0:T(8,128)S(1)}, f32[16,64,128]{2,1,0:T(8,128)S(1)}, u32[]{:S(2)}, u32[]{:S(2)}) collective-permute-start(f32[16,64,128]{2,1,0:T(8,128)S(1)} %copy-done.13), channel_id=1, source_target_pairs={{0,224},{4,228},{8,232},{12,236},{16,240},{20,244},{24,248},{28,25... | collective-permute-start | bytes 1572872 | tf_op jit(solution)/shard_map/ppermute | solution.py:26
  290.7 13.0 %collective-permute-start.37 = (f32[16,64,128]{2,1,0:T(8,128)S(1)}, f32[16,64,128]{2,1,0:T(8,128)S(1)}, u32[]{:S(2)}, u32[]{:S(2)}) collective-permute-start(f32[16,64,128]{2,1,0:T(8,128)S(1)} %collective-permute-done.32.refs_0_), channel_id=1, source_target_pairs={{0,32},{4,36},{8,40},{12,44},{16,48},{20,52},{24,56},{28,60},{32,6... | collective-permute-start | bytes 1572872 | tf_op jit(solution)/shard_map/ppermute | solution.py:26
  298.3 12.8 %collective-permute-start.38 = (f32[16,64,128]{2,1,0:T(8,128)S(1)}, f32[16,64,128]{2,1,0:T(8,128)S(1)}, u32[]{:S(2)}, u32[]{:S(2)}) collective-permute-start(f32[16,64,128]{2,1,0:T(8,128)S(1)} %collective-permute-done.33.refs_1_), channel_id=1, source_target_pairs={{0,224},{4,228},{8,232},{12,236},{16,240},{20,244},{24,248},{28,25... | collective-permute-start | bytes 1572872 | tf_op jit(solution)/shard_map/ppermute | solution.py:26
  303.6 12.2 %collective-permute-start.39 = (f32[16,64,128]{2,1,0:T(8,128)S(1)}, f32[16,64,128]{2,1,0:T(8,128)}, u32[]{:S(2)}, u32[]{:S(2)}) collective-permute-start(f32[16,64,128]{2,1,0:T(8,128)S(1)} %collective-permute-done.37.refs_0_), channel_id=1, source_target_pairs={{0,32},{4,36},{8,40},{12,44},{16,48},{20,52},{24,56},{28,60},{32,6... | collective-permute-start | bytes 1572872 | tf_op jit(solution)/shard_map/ppermute | solution.py:26
  321.2 79.4 %all-to-all-start.3 = ((f32[4,24,64,128]{3,2,1,0:T(8,128)}), f32[4,24,64,128]{3,2,1,0:T(8,128)S(1)}, u32[]{:S(2)}, u32[]{:S(2)}) async-start(f32[4,24,64,128]{3,2,1,0:T(8,128)} %pack.13), calls=%async_computation.3 | async-start | bytes 6291456 | tf_op jit(solution)/shard_map/all_to_all | solution.py:35
  326.5 49.6 %collective-permute-start.27 = (f32[8,64,128]{2,1,0:T(8,128)}, f32[8,64,128]{2,1,0:T(8,128)S(1)}, u32[]{:S(2)}, u32[]{:S(2)}) collective-permute-start(f32[8,64,128]{2,1,0:T(8,128)} %get-tuple-element.31), channel_id=1, source_target_pairs={{0,8},{4,12},{8,16},{12,20},{16,24},{20,28},{24,0},{28,4},{32,40},... | collective-permute-start | bytes 786440 | tf_op jit(solution)/shard_map/ppermute | solution.py:26
  328.7 48.2 %collective-permute-start.28 = (f32[8,64,128]{2,1,0:T(8,128)}, f32[8,64,128]{2,1,0:T(8,128)}, u32[]{:S(2)}, u32[]{:S(2)}) collective-permute-start(f32[8,64,128]{2,1,0:T(8,128)} %get-tuple-element.32), channel_id=1, source_target_pairs={{0,16},{4,20},{8,24},{12,28},{16,0},{20,4},{24,8},{28,12},{32,48},... | collective-permute-start | bytes 786440 | tf_op jit(solution)/shard_map/ppermute | solution.py:26
  334.6 59.2 %collective-permute-start.34 = (f32[16,64,128]{2,1,0:T(8,128)}, f32[16,64,128]{2,1,0:T(8,128)}, u32[]{:S(2)}, u32[]{:S(2)}) collective-permute-start(f32[16,64,128]{2,1,0:T(8,128)} %get-tuple-element.36), channel_id=1, source_target_pairs={{0,8},{4,12},{8,16},{12,20},{16,24},{20,28},{24,0},{28,4},{32,40},... | collective-permute-start | bytes 1572872 | tf_op jit(solution)/shard_map/ppermute | solution.py:26
  334.6 60.1 %collective-permute-start.35 = (f32[16,64,128]{2,1,0:T(8,128)}, f32[16,64,128]{2,1,0:T(8,128)}, u32[]{:S(2)}, u32[]{:S(2)}) collective-permute-start(f32[16,64,128]{2,1,0:T(8,128)} %get-tuple-element.37), channel_id=1, source_target_pairs={{0,16},{4,20},{8,24},{12,28},{16,0},{20,4},{24,8},{28,12},{32,48},... | collective-permute-start | bytes 1572872 | tf_op jit(solution)/shard_map/ppermute | solution.py:26
  376.1 18.6 %collective-permute-start.36 = (f32[16,64,128]{2,1,0:T(8,128)}, f32[16,64,128]{2,1,0:T(8,128)}, u32[]{:S(2)}, u32[]{:S(2)}) collective-permute-start(f32[16,64,128]{2,1,0:T(8,128)} %get-tuple-element.38), channel_id=1, source_target_pairs={{0,24},{4,28},{8,0},{12,4},{16,8},{20,12},{24,16},{28,20},{32,56},... | collective-permute-start | bytes 1572872 | tf_op jit(solution)/shard_map/ppermute | solution.py:26
  376.9 16.9 %collective-permute-start.29 = (f32[8,64,128]{2,1,0:T(8,128)}, f32[8,64,128]{2,1,0:T(8,128)}, u32[]{:S(2)}, u32[]{:S(2)}) collective-permute-start(f32[8,64,128]{2,1,0:T(8,128)} %get-tuple-element.33), channel_id=1, source_target_pairs={{0,24},{4,28},{8,0},{12,4},{16,8},{20,12},{24,16},{28,20},{32,56},... | collective-permute-start | bytes 786440 | tf_op jit(solution)/shard_map/ppermute | solution.py:26
  417.2 1.6 collective-permute-start.40
  (20 other events, 268.3 us)
